TPU v7x, 32 devices: a whole 2x2x4 slice. The times are simulated.
32 devices in a mesh: span: 4 (over y, x), tensor: 8 (over z, core).
Axes of the slice: x: 2, y: 2, z: 4, core: 2. Of those that a mesh axis runs over, the one named last changes fastest.
Arguments:
- tokens: bfloat16 [1024, 4096], P('span', 'tensor'), may hold values from -200 to 200
- retain: float32 [1024], P('span'), may hold values from 0.5 to 1
- norm_gain: float32 [4096], P('tensor'), may hold values from 0.1 to 1.9
- norm_bias: float32 [4096], P('tensor'), may hold values from -2.5 to 2.5
- decay_rate: float32 [16, 4096], P(None, 'tensor'), may hold values from 0.00024414062 to 0.0333333333
- ema_angle: float32 [16, 4096], P(None, 'tensor'), may hold values from -0.05 to 0.05
- ema_input: float32 [16, 4096], P(None, 'tensor'), may hold values from -2.4 to 2.4
- ema_output: float32 [2, 16, 4096], P(None, None, 'tensor'), may hold values from -0.25 to 0.25
- ema_skip: float32 [4096], P('tensor'), may hold values from -3 to 3
- shared_weight: bfloat16 [4096, 1024], P('tensor'), may hold values from -0.125 to 0.125
- shared_gain: float32 [1024], replicated, may hold values from 0.1 to 1.9
- output_weight: bfloat16 [1024, 4096], P(None, 'tensor'), may hold values from -0.1875 to 0.1875
Outputs:
- layer_out: bfloat16 [1024, 4096], P('span', 'tensor')
All inputs are finite; a program needn't handle non-finite values.
Results may differ from a plain program's by a relative error of at most 0.02.
Values may be sent and summed in bfloat16 or wider, within the bound.
A program may use at most 128 MiB of HBM per device.

v0:
```python
import jax
import jax.numpy as jnp
from jax import lax
from jax.sharding import PartitionSpec as P

GROUP = 64
BLOCK = 64


precise = lax.Precision.HIGHEST
norm_eps = 1e-05
scale_eps = 1e-06


def shifted(shard, axis, by):
    length = lax.axis_size(axis)
    pairs = [(i, i + by) for i in range(length) if 0 <= i + by < length]
    return lax.ppermute(shard, axis, pairs)


def lag_powers(decay_rate, ema_angle, count):
    lag_steps = jnp.arange(count, dtype=jnp.int32).astype(jnp.float32)[:, None, None]
    magnitude = jnp.exp(-decay_rate[None] * lag_steps)
    return (
        magnitude * jnp.cos(ema_angle[None] * lag_steps),
        magnitude * jnp.sin(ema_angle[None] * lag_steps),
    )


def toeplitz(kernel):
    width = kernel.shape[0]
    flipped = jnp.concatenate([kernel[::-1], jnp.zeros_like(kernel)], axis=0)
    repeated = jnp.tile(flipped, (width, 1))[: width * (2 * width - 1)]
    return repeated.reshape(width, 2 * width - 1, kernel.shape[1])[:, width - 1 : 2 * width - 1]


def block_combine(earlier, later):
    mult_re = later[0] * earlier[0] - later[1] * earlier[1]
    mult_im = later[0] * earlier[1] + later[1] * earlier[0]
    add_re = later[0] * earlier[2] - later[1] * earlier[3] + later[2]
    add_im = later[0] * earlier[3] + later[1] * earlier[2] + later[3]
    return (mult_re, mult_im, add_re, add_im)


def group_terms(tokens):
    values = tokens.astype(jnp.float32)
    grouped = values.reshape(values.shape[0], -1, GROUP)
    return (grouped, jnp.sum(grouped, axis=2), jnp.sum(grouped * grouped, axis=2))


def timestep_norm(grouped, group_sums, group_squares, before, first_row, norm_gain, norm_bias):
    length = grouped.shape[0]
    cum_sum = before[0][None] + jnp.cumsum(group_sums, axis=0)
    cum_sq = before[1][None] + jnp.cumsum(group_squares, axis=0)
    counts = ((first_row + jnp.arange(length, dtype=jnp.int32) + 1) * GROUP).astype(jnp.float32)[
        :, None
    ]
    average = cum_sum / counts
    spread = cum_sq / counts - average * average
    inverse = lax.rsqrt(spread + norm_eps)
    normed = (grouped - average[:, :, None]) * inverse[:, :, None]
    return normed.reshape(length, -1) * norm_gain[None] + norm_bias[None]


def ema_local(normed, retain, decay_rate, ema_angle, ema_input, ema_output):
    length, channels = normed.shape
    blocks = length // BLOCK
    power_real, power_im = lag_powers(decay_rate, ema_angle, BLOCK + 1)
    weight = (1.0 - jnp.exp(-decay_rate)) * ema_input
    kernel = jnp.sum(
        weight[None]
        * (ema_output[0][None] * power_real[:BLOCK] - ema_output[1][None] * power_im[:BLOCK]),
        axis=1,
    )
    matrix = toeplitz(kernel)
    retained = jnp.cumprod(retain.reshape(blocks, BLOCK), axis=1)
    scaled = normed.reshape(blocks, BLOCK, channels) / retained[:, :, None]
    within = jnp.einsum("tsd,bsd->btd", matrix, scaled, precision=precise)
    back_re = power_real[:BLOCK][::-1]
    back_im = power_im[:BLOCK][::-1]
    end_re = weight[None] * jnp.einsum("bsd,sjd->bjd", scaled, back_re, precision=precise)
    end_im = weight[None] * jnp.einsum("bsd,sjd->bjd", scaled, back_im, precision=precise)
    closing = retained[:, -1][:, None, None]
    elements = (
        closing * power_real[BLOCK][None],
        closing * power_im[BLOCK][None],
        closing * end_re,
        closing * end_im,
    )
    return (within, retained, elements, (power_real, power_im))


def ema_finish(within, retained, prior_re, prior_im, powers, ema_output, normed, ema_skip):
    power_real, power_im = powers
    multiplier_cosine_part = (
        ema_output[0][None] * power_real[1:] - ema_output[1][None] * power_im[1:]
    )
    coeff_im = ema_output[0][None] * power_im[1:] + ema_output[1][None] * power_real[1:]
    carried_part = jnp.einsum(
        "bjd,tjd->btd", prior_re, multiplier_cosine_part, precision=precise
    ) - jnp.einsum("bjd,tjd->btd", prior_im, coeff_im, precision=precise)
    mixed = retained[:, :, None] * (within + carried_part)
    return mixed.reshape(normed.shape) + ema_skip[None] * normed


def shards(
    tokens,
    retain,
    norm_gain,
    norm_bias,
    decay_rate,
    ema_angle,
    ema_input,
    ema_output,
    ema_skip,
    shared_weight,
    shared_gain,
    output_weight,
):
    length = tokens.shape[0]
    interval_number = lax.axis_size("span")
    grouped, group_sums, group_squares = group_terms(tokens)
    local_stats = jnp.stack([jnp.sum(group_sums, axis=0), jnp.sum(group_squares, axis=0)])

    def stat_turn(turn_index, carried):
        return shifted(carried + local_stats, "span", 1)

    before = lax.fori_loop(0, interval_number - 1, stat_turn, jnp.zeros_like(local_stats))
    first_row = lax.axis_index("span") * length
    normed = timestep_norm(
        grouped, group_sums, group_squares, before, first_row, norm_gain, norm_bias
    )
    within, retained, elements, powers = ema_local(
        normed, retain, decay_rate, ema_angle, ema_input, ema_output
    )
    inclusive = lax.associative_scan(block_combine, elements)
    summary = tuple((member[-1] for member in inclusive))

    def state_turn(turn_index, carried):
        moved_re = summary[0] * carried[0] - summary[1] * carried[1] + summary[2]
        moved_im = summary[0] * carried[1] + summary[1] * carried[0] + summary[3]
        return shifted(jnp.stack([moved_re, moved_im]).astype(jnp.bfloat16), "span", 1).astype(
            jnp.float32
        )

    incoming_state = lax.fori_loop(
        0, interval_number - 1, state_turn, jnp.zeros((2,) + summary[0].shape, jnp.float32)
    )
    state_re = incoming_state[0]
    state_im = incoming_state[1]
    mult_re = jnp.concatenate([jnp.ones_like(inclusive[0][:1]), inclusive[0][:-1]], axis=0)
    mult_im = jnp.concatenate([jnp.zeros_like(inclusive[1][:1]), inclusive[1][:-1]], axis=0)
    local_re = jnp.concatenate([jnp.zeros_like(inclusive[2][:1]), inclusive[2][:-1]], axis=0)
    local_im = jnp.concatenate([jnp.zeros_like(inclusive[3][:1]), inclusive[3][:-1]], axis=0)
    prior_re = mult_re * state_re[None] - mult_im * state_im[None] + local_re
    prior_im = mult_re * state_im[None] + mult_im * state_re[None] + local_im
    ema = ema_finish(within, retained, prior_re, prior_im, powers, ema_output, normed, ema_skip)
    active = jax.nn.silu(ema).astype(jnp.bfloat16)
    shared_part = lax.psum_scatter(
        jnp.dot(active, shared_weight, preferred_element_type=jnp.float32).astype(jnp.bfloat16),
        "tensor",
        scatter_dimension=0,
        tiled=True,
    ).astype(jnp.float32)
    squares = jnp.mean(shared_part * shared_part, axis=1, keepdims=True)
    common_rescaled = (shared_part * lax.rsqrt(squares + scale_eps) * shared_gain[None]).astype(
        jnp.bfloat16
    )
    mixed = jnp.dot(
        lax.all_gather(common_rescaled, "tensor", axis=0, tiled=True),
        output_weight,
        preferred_element_type=jnp.float32,
    )
    return mixed.astype(jnp.bfloat16)


def solution(mesh):
    in_specs = (
        P("span", "tensor"),
        P("span"),
        P("tensor"),
        P("tensor"),
        P(None, "tensor"),
        P(None, "tensor"),
        P(None, "tensor"),
        P(None, None, "tensor"),
        P("tensor"),
        P("tensor", None),
        P(),
        P(None, "tensor"),
    )
    out_specs = P("span", "tensor")
    return jax.shard_map(shards, mesh=mesh, in_specs=in_specs, out_specs=out_specs, check_vma=False)
```

profile of v0, /device:TPU:7, one launch (start us, length us, event | category | flops | bytes accessed | tf_op | source)
XLA Modules:
  0.0 2272.6 jit_solution(15256299274504939504)
XLA Ops:
  8.5 13.6 while.21
  9.8 3.0 collective-permute-done
  14.1 3.0 collective-permute-done
  18.5 3.6 collective-permute-done
  27.0 8.6 fusion.4
  35.6 4.7 multiply_add_fusion
  40.3 3.2 rev.11
  43.5 5.4 copy.100
  49.5 10.3 fusion.9
  59.8 10.1 slice.236
  69.9 10.1 slice.233
  80.0 3.2 rev.10
  83.2 5.6 copy.98
  88.9 10.3 fusion.11
  99.2 10.1 slice.232
  109.3 10.1 slice.234
  121.2 1.4 broadcast_multiply_fusion.1
  122.5 6.7 slice.218
  129.2 6.7 slice.219
  135.9 6.7 slice.215
  142.6 6.7 slice.216
  149.3 2.9 fusion.60
  152.1 2.4 add_add_fusion
  155.1 1.7 multiply_subtract_fusion.2
  158.2 2.2 slice_multiply_fusion.3
  160.4 3.1 fusion.61
  168.1 152.6 %pad.95 = f32[3,16,512]{1,0,2:T(4,128)} pad(f32[2,16,512]{1,0,2:T(2,128)S(1)} %copy.109, f32[]{:T(128)} %constant.20.clone.1), padding=0_0_1x0_0_0x0_0_0 | pad | bytes 163844 | tf_op jit(solution)/shard_map/slice | solution.py:154
  320.7 152.5 %pad.71 = f32[4,16,512]{1,0,2:T(4,128)} pad(f32[2,16,512]{1,0,2:T(2,128)S(1)} %copy.109, f32[]{:T(128)} %constant.20.clone.1), padding=0_1_1x0_0_0x0_0_0 | pad | bytes 196612 | tf_op jit(solution)/shard_map/pad | solution.py:136
  473.3 2.3 pad_add_fusion.1
  475.6 2.9 fusion.63
  480.3 152.4 %pad.144 = f32[3,16,512]{1,0,2:T(4,128)} pad(f32[2,16,512]{1,0,2:T(2,128)S(1)} %pad_add_fusion.3, f32[]{:T(128)} %constant.20.clone.1), padding=0_0_1x0_0_0x0_0_0 | pad | bytes 163844
  632.8 151.1 %pad.62 = f32[4,16,512]{1,0,2:T(4,128)} pad(f32[2,16,512]{1,0,2:T(2,128)S(1)} %pad_add_fusion.3, f32[]{:T(128)} %constant.20.clone.1), padding=1_0_1x0_0_0x0_0_0 | pad | bytes 196612 | tf_op jit(solution)/shard_map/pad | solution.py:136
  786.2 151.5 %pad.63 = f32[4,16,512]{1,0,2:T(4,128)} pad(f32[2,16,512]{1,0,2:T(2,128)S(1)} %copy.96, f32[]{:T(128)} %constant.20.clone.1), padding=0_1_1x0_0_0x0_0_0 | pad | bytes 196612 | tf_op jit(solution)/shard_map/pad | solution.py:136
  937.7 152.6 %pad.91 = f32[3,16,512]{1,0,2:T(4,128)} pad(f32[2,16,512]{1,0,2:T(2,128)S(1)} %copy.96, f32[]{:T(128)} %constant.20.clone.1), padding=0_0_1x0_0_0x0_0_0 | pad | bytes 163844 | tf_op jit(solution)/shard_map/slice | solution.py:152
  1091.0 152.9 %pad.69 = f32[4,16,512]{1,0,2:T(4,128)} pad(f32[2,16,512]{1,0,2:T(2,128)S(1)} %copy.104, f32[]{:T(128)} %constant.20.clone.1), padding=0_1_1x0_0_0x0_0_0 | pad | bytes 196612 | tf_op jit(solution)/shard_map/pad | solution.py:136
  1243.9 152.8 %pad.93 = f32[3,16,512]{1,0,2:T(4,128)} pad(f32[2,16,512]{1,0,2:T(2,128)S(1)} %copy.104, f32[]{:T(128)} %constant.20.clone.1), padding=0_0_1x0_0_0x0_0_0 | pad | bytes 163844 | tf_op jit(solution)/shard_map/slice | solution.py:153
  1396.7 170.7 %pad.72 = f32[4,16,512]{1,0,2:T(4,128)S(1)} pad(f32[2,16,512]{1,0,2:T(2,128)} %pad_add_fusion, f32[]{:T(128)} %constant.20.clone.1), padding=1_0_1x0_0_0x0_0_0 | pad | bytes 196612 | tf_op jit(solution)/shard_map/pad | solution.py:136
  1568.6 1.7 slice_add_fusion.1
  1570.4 170.7 %pad.141 = f32[4,16,512]{1,0,2:T(4,128)S(1)} pad(f32[2,16,512]{1,0,2:T(2,128)} %pad_add_fusion.1, f32[]{:T(128)} %constant.20.clone.1), padding=1_0_1x0_0_0x0_0_0 | pad | bytes 196612
  1741.1 1.7 slice_add_fusion.2
  1742.9 171.1 %pad.142 = f32[4,16,512]{1,0,2:T(4,128)S(1)} pad(f32[2,16,512]{1,0,2:T(2,128)} %pad_add_fusion.2, f32[]{:T(128)} %constant.20.clone.1), padding=1_0_1x0_0_0x0_0_0 | pad | bytes 196612
  1913.9 2.8 slice_add_fusion.5
  1917.8 2.2 slice.380
  1921.0 17.2 while.22
  1922.4 4.3 collective-permute-done.1
  1928.0 4.3 collective-permute-done.1
  1933.6 4.6 collective-permute-done.1
  1942.6 152.6 %pad.61 = f32[4,16,512]{1,0,2:T(4,128)} pad(f32[2,16,512]{1,0,2:T(2,128)S(1)} %copy.92, f32[]{:T(128)} %constant.20.clone.1), padding=0_1_1x0_0_0x0_0_0 | pad | bytes 196612 | tf_op jit(solution)/shard_map/pad | solution.py:136
  2095.2 1.9 slice_add_fusion.7
  2098.4 5.5 copy.116
  2104.0 2.1 tile.4
  2106.2 6.1 slice.260
  2112.3 14.1 reshape.96
  2126.4 8.6 slice.261
  2135.0 16.3 copy.120
  2151.3 29.1 %convolution_bitcast_fusion.2 = f32[4,64,512]{1,0,2:T(4,128)S(1)} fusion(f32[64,64,512]{1,0,2:T(8,128)} %copy.120, f32[4,64,512]{1,0,2:T(4,128)} %copy.85, f32[4,64]{1,0:T(4,128)S(1)} %reduce_window.9), kind=kOutput, calls=%fused_computation.30 | convolution fusion | flops 100794368 | bytes 9438208 | tf_op jit(solution)/shard_map/tsd,bsd->btd/dot_general | solution.py:78
  2180.3 5.3 copy.117
  2185.6 1.9 slice_add_fusion
  2187.5 7.2 fusion.18
  2194.7 6.1 fusion.12
  2200.8 1.6 copy.118
  2203.5 2.6 convolution_convert_fusion
  2206.1 37.5 %reduce-scatter.2.cloned.1.call-done = bf16[32,1024]{1,0:T(8,128)(2,1)} async-done(((bf16[256,1024]{1,0:T(8,128)(2,1)}), bf16[32,1024]{1,0:T(8,128)(2,1)}) %reduce-scatter.2.cloned.1.call-update) | async-done | bytes 65552 | tf_op jit(solution)/shard_map/reduce_scatter | solution.py:159
  2245.5 18.6 all_gather.3
  (172 shorter events, 41.4 us)
Async XLA Ops:
  6.5 2196.9 %copy-start = (bf16[512,1024]{1,0:T(8,128)(2,1)S(1)}, bf16[512,1024]{1,0:T(8,128)(2,1)}, u32[]{:S(2)}) copy-start(bf16[512,1024]{1,0:T(8,128)(2,1)} %param.25) | copy-start | bytes 3145732
  6.5 2237.1 %reduce-scatter.2.cloned.1.call-start = ((), (), s32[]{:S(2)}) async-start(), calls=%async_computation.1 | async-start | bytes 589824 | tf_op jit(solution)/shard_map/reduce_scatter | solution.py:159
  7.7 18.5 copy-start.27
  7.7 18.5 copy-start.28
  7.7 18.5 copy-start.29
  8.5 4.3 collective-permute-start
  12.9 4.3 collective-permute-start
  17.2 4.9 collective-permute-start
  24.6 2.3 copy-start.18
  35.5 4.7 copy-start.1
  43.5 5.5 copy-start.31
  154.9 3.3 copy-start.9
  155.1 5.3 copy-start.14
  156.9 6.7 copy-start.11
  156.9 6.7 copy-start.13
  156.9 6.7 copy-start.16
  166.8 306.5 %copy-start.10 = (f32[1,16,512]{1,0,2:T(1,128)S(1)}, f32[1,16,512]{1,0,2:T(1,128)}, u32[]{:S(2)}) copy-start(f32[1,16,512]{1,0,2:T(1,128)} %copy-done.9) | copy-start | bytes 98308
  320.7 157.7 %copy-start.12 = (f32[1,16,512]{1,0,2:T(1,128)S(1)}, f32[1,16,512]{1,0,2:T(1,128)}, u32[]{:S(2)}) copy-start(f32[1,16,512]{1,0,2:T(1,128)} %copy-done.11) | copy-start | bytes 98308
  473.3 6.5 copy-start.15
  473.3 6.5 copy-start.17
  479.8 304.1 %copy-start.23 = (f32[1,16,512]{1,0,2:T(1,128)S(1)}, f32[1,16,512]{1,0,2:T(1,128)}, u32[]{:S(2)}) copy-start(f32[1,16,512]{1,0,2:T(1,128)} %get-tuple-element.152) | copy-start | bytes 98308
  479.8 304.1 %copy-start.24 = (f32[1,16,512]{1,0,2:T(1,128)S(1)}, f32[1,16,512]{1,0,2:T(1,128)}, u32[]{:S(2)}) copy-start(f32[1,16,512]{1,0,2:T(1,128)} %get-tuple-element.154) | copy-start | bytes 98308
  785.9 304.5 %copy-start.25 = (f32[1,16,512]{1,0,2:T(1,128)S(1)}, f32[1,16,512]{1,0,2:T(1,128)}, u32[]{:S(2)}) copy-start(f32[1,16,512]{1,0,2:T(1,128)} %get-tuple-element.150) | copy-start | bytes 98308
  785.9 304.6 %copy-start.22 = (f32[1,16,512]{1,0,2:T(1,128)S(1)}, f32[1,16,512]{1,0,2:T(1,128)}, u32[]{:S(2)}) copy-start(f32[1,16,512]{1,0,2:T(1,128)} %get-tuple-element.165) | copy-start | bytes 98308
  786.2 304.4 %copy-start.21 = (f32[1,16,512]{1,0,2:T(1,128)S(1)}, f32[1,16,512]{1,0,2:T(1,128)}, u32[]{:S(2)}) copy-start(f32[1,16,512]{1,0,2:T(1,128)} %get-tuple-element.164) | copy-start | bytes 98308
  1091.0 476.4 %copy-start.7 = (f32[3,16,512]{1,0,2:T(4,128)S(1)}, f32[3,16,512]{1,0,2:T(4,128)}, u32[]{:S(2)}) copy-start(f32[3,16,512]{1,0,2:T(4,128)} %pad.95) | copy-start | bytes 294916
  1913.9 7.1 copy-start.3
  1921.1 5.6 collective-permute-start.1
  1926.7 5.6 collective-permute-start.1
  1932.3 5.9 collective-permute-start.1
  2095.2 1.9 copy-start.6
  2098.4 5.5 copy-start.26
  2185.6 1.9 copy-start.5
  2185.6 1.9 copy-start.8
  2187.5 7.2 copy-start.2
  2187.5 7.2 copy-start.4
  2200.8 2.6 copy-start.19
  2200.8 2.6 copy-start.32
  2203.5 41.1 %copy-start.30 = (f32[1024]{0:T(1024)S(1)}, f32[1024]{0:T(1024)}, u32[]{:S(2)}) copy-start(f32[1024]{0:T(1024)} %param.26) | copy-start | bytes 12292
  2203.5 60.7 %copy-start.20 = (bf16[1024,512]{1,0:T(8,128)(2,1)S(1)}, bf16[1024,512]{1,0:T(8,128)(2,1)}, u32[]{:S(2)}) copy-start(bf16[1024,512]{1,0:T(8,128)(2,1)} %param.27) | copy-start | bytes 3145732
Sparse Core Ops, SparseCore 0:
  2206.2 37.3 reduce-scatter.1
where the time goes:
time: 2300 us; the launch traced here: 2270 us
  local copies, waits for them, and re-layouts  2060 us (90%)
  matrix products  66.7 us (3%)
  waiting for transfers between devices  60.3 us (3%)
  other arithmetic  48.6 us (2%)
    pad x6, local copies, waits for them, and re-layouts, shards(): inclusive = lax.associative_scan(block_combine, elements)  931 us
    unnamed x81, local copies, waits for them, and re-layouts  518 us
    slice x1, local copies, waits for them, and re-layouts, shards(): inclusive[2][:-1]  153 us
    slice x1, local copies, waits for them, and re-layouts, shards(): inclusive[3][:-1]  153 us
    slice x1, local copies, waits for them, and re-layouts, shards(): inclusive[1][:-1]  153 us
    slice x13, local copies, waits for them, and re-layouts, shards(): inclusive = lax.associative_scan(block_combine, elements)  73.5 us
  transfers between devices with their start and end apart: 7, of which 7 were waited for; matrix products, arithmetic and copies ran while one was open for 0% of the time, Pallas kernels for 0%

commit v1 on v0

v1 whole, which is shorter than its diff:
```python
import functools

import jax
import jax.numpy as jnp
from jax import lax
from jax.experimental import pallas as pl
from jax.experimental.pallas import tpu as pltpu
from jax.sharding import PartitionSpec as P

GROUP = 64
STEPS = 8
NORM_EPS = 1e-05
SCALE_EPS = 1e-06

VMEM = pl.BlockSpec(memory_space=pltpu.VMEM)
SMEM = pl.BlockSpec(memory_space=pltpu.SMEM)


def dot(a, b):
    return jnp.dot(a, b, preferred_element_type=jnp.float32)


def pieces(values, count):
    out = []
    for _ in range(count):
        piece = values.astype(jnp.bfloat16)
        out.append(piece)
        values = values - piece.astype(jnp.float32)
    return out


def group_ones(channels):
    row = lax.broadcasted_iota(jnp.int32, (channels, channels), 0) // GROUP
    column = lax.broadcasted_iota(jnp.int32, (channels, channels), 1) // GROUP
    return (row == column).astype(jnp.bfloat16)


def stats_kernel(tokens_ref, retain_ref, stats_ref):
    length, channels = tokens_ref.shape
    values = tokens_ref[...].astype(jnp.float32)
    total = jnp.sum(values, axis=0, keepdims=True)
    squares = jnp.sum(values * values, axis=0, keepdims=True)
    rows = jnp.concatenate([total, squares, jnp.zeros((6, channels), jnp.float32)], axis=0)
    ones = group_ones(channels)
    grouped = sum(dot(piece, ones) for piece in pieces(rows, 3))
    kept = retain_ref[...]
    while kept.shape[0] > 1:
        half = kept.shape[0] // 2
        kept = kept[:half] * kept[half:]
    row = lax.broadcasted_iota(jnp.int32, (8, channels), 0)
    stats_ref[...] = jnp.where(row == 2, jnp.broadcast_to(kept, (8, channels)), grouped)


def span_stats(tokens, retain):
    return pl.pallas_call(
        stats_kernel,
        out_shape=jax.ShapeDtypeStruct((8, tokens.shape[1]), jnp.float32),
        in_specs=[VMEM, VMEM],
        out_specs=VMEM,
        name="span_stats",
    )(tokens, retain.reshape(-1, 1))


def local_kernel(tokens_ref, stats_ref, retain_ref, gain_ref, bias_ref, rate_ref, angle_ref, normed_ref, state_ref):
    length, channels = tokens_ref.shape
    ndim = rate_ref.shape[0]
    me = lax.axis_index("span")
    before = jnp.zeros((8, channels), jnp.float32)
    for other in range(stats_ref.shape[0]):
        before = before + jnp.where(other < me, stats_ref[other], 0.0)
    tokens = tokens_ref[...]
    values = tokens.astype(jnp.float32)
    ones = group_ones(channels)
    sums = dot(tokens, ones)
    squares = sum(dot(piece, ones) for piece in pieces(values * values, 2))
    row = lax.broadcasted_iota(jnp.int32, (length, length), 0)
    column = lax.broadcasted_iota(jnp.int32, (length, length), 1)
    lower = (column <= row).astype(jnp.bfloat16)
    cum_sum = before[0:1] + sum(dot(lower, piece) for piece in pieces(sums, 3))
    cum_sq = before[1:2] + sum(dot(lower, piece) for piece in pieces(squares, 3))
    position = lax.broadcasted_iota(jnp.int32, (length, channels), 0)
    counts = ((me * length + position + 1) * GROUP).astype(jnp.float32)
    average = cum_sum / counts
    spread = cum_sq / counts - average * average
    inverse = lax.rsqrt(spread + NORM_EPS)
    normed_ref[...] = (values - average) * inverse * gain_ref[...] + bias_ref[...]

    width = min(256, channels)
    for start in range(0, channels, width):
        lanes = slice(start, start + width)
        size = jnp.exp(-rate_ref[:, lanes])
        turn_re = size * jnp.cos(angle_ref[:, lanes])
        turn_im = size * jnp.sin(angle_ref[:, lanes])

        def steps(block, carried):
            re, im = carried
            first = pl.multiple_of(block * STEPS, STEPS)
            for step in range(STEPS):
                entry = normed_ref[pl.ds(first + step, 1), lanes]
                keep = retain_ref[first + step]
                re, im = (
                    (turn_re * re - turn_im * im) * keep + entry,
                    (turn_re * im + turn_im * re) * keep,
                )
            return re, im

        zero = jnp.zeros((ndim, width), jnp.float32)
        re, im = lax.fori_loop(0, length // STEPS, steps, (zero, zero))
        state_ref[0:ndim, lanes] = re.astype(state_ref.dtype)
        state_ref[ndim:, lanes] = im.astype(state_ref.dtype)


def local_scan(tokens, stats, retain, gain, bias, rate, angle):
    length, channels = tokens.shape
    return pl.pallas_call(
        local_kernel,
        out_shape=(
            jax.ShapeDtypeStruct((length, channels), jnp.float32),
            jax.ShapeDtypeStruct((2 * rate.shape[0], channels), jnp.bfloat16),
        ),
        in_specs=[VMEM, VMEM, SMEM, VMEM, VMEM, VMEM, VMEM],
        out_specs=(VMEM, VMEM),
        name="local_scan",
    )(tokens, stats, retain, gain.reshape(1, -1), bias.reshape(1, -1), rate, angle)


def full_kernel(normed_ref, states_ref, stats_ref, retain_ref, rate_ref, angle_ref, input_ref, output_ref, skip_ref, weight_ref, part_ref, ema_ref):
    length, channels = normed_ref.shape
    ndim = rate_ref.shape[0]
    me = lax.axis_index("span")
    width = min(256, channels)
    for start in range(0, channels, width):
        lanes = slice(start, start + width)
        rate, angle = rate_ref[:, lanes], angle_ref[:, lanes]
        size = jnp.exp(-rate)
        turn_re = size * jnp.cos(angle)
        turn_im = size * jnp.sin(angle)
        weight = (1.0 - size) * input_ref[:, lanes]
        read_re = weight * output_ref[0, :, lanes]
        read_im = weight * output_ref[1, :, lanes]
        whole = jnp.exp(-rate * length)
        whole_re = whole * jnp.cos(angle * length)
        whole_im = whole * jnp.sin(angle * length)
        re = jnp.zeros((ndim, width), jnp.float32)
        im = jnp.zeros((ndim, width), jnp.float32)
        for other in range(states_ref.shape[0]):
            keep = stats_ref[other, 2:3, lanes]
            here_re = states_ref[other, 0:ndim, lanes].astype(jnp.float32)
            here_im = states_ref[other, ndim:, lanes].astype(jnp.float32)
            next_re = (whole_re * re - whole_im * im) * keep + here_re
            next_im = (whole_re * im + whole_im * re) * keep + here_im
            re = jnp.where(other < me, next_re, re)
            im = jnp.where(other < me, next_im, im)

        def steps(block, carried):
            re, im = carried
            first = pl.multiple_of(block * STEPS, STEPS)
            for step in range(STEPS):
                entry = normed_ref[pl.ds(first + step, 1), lanes]
                keep = retain_ref[first + step]
                re, im = (
                    (turn_re * re - turn_im * im) * keep + entry,
                    (turn_re * im + turn_im * re) * keep,
                )
                ema_ref[pl.ds(first + step, 1), lanes] = jnp.sum(read_re * re - read_im * im, axis=0, keepdims=True)
            return re, im

        lax.fori_loop(0, length // STEPS, steps, (re, im))
    ema = ema_ref[...] + skip_ref[...] * normed_ref[...]
    active = (ema / (1.0 + jnp.exp(-ema))).astype(jnp.bfloat16)
    part_ref[...] = dot(active, weight_ref[...]).astype(jnp.bfloat16)


def full_scan(normed, states, stats, retain, rate, angle, source, output, skip, weight):
    length, channels = normed.shape
    return pl.pallas_call(
        full_kernel,
        out_shape=jax.ShapeDtypeStruct((length, weight.shape[1]), jnp.bfloat16),
        in_specs=[VMEM, VMEM, VMEM, SMEM] + [VMEM] * 6,
        out_specs=VMEM,
        scratch_shapes=[pltpu.VMEM((length, channels), jnp.float32)],
        name="full_scan",
    )(normed, states, stats, retain, rate, angle, source, output, skip.reshape(1, -1), weight)


def span_gather(values):
    return lax.all_gather(values, "span", axis=0)


def mix(part, gain):
    shared = lax.psum_scatter(part, "tensor", scatter_dimension=0, tiled=True).astype(jnp.float32)
    squares = jnp.mean(shared * shared, axis=1, keepdims=True)
    normed = (shared * lax.rsqrt(squares + SCALE_EPS) * gain[None]).astype(jnp.bfloat16)
    return lax.all_gather(normed, "tensor", axis=0, tiled=True)


def shards(tokens, retain, norm_gain, norm_bias, decay_rate, ema_angle, ema_input, ema_output, ema_skip, shared_weight, shared_gain, output_weight):
    stats = span_gather(span_stats(tokens, retain))
    normed, state = local_scan(tokens, stats, retain, norm_gain, norm_bias, decay_rate, ema_angle)
    states = span_gather(state)
    part = full_scan(normed, states, stats, retain, decay_rate, ema_angle, ema_input, ema_output, ema_skip, shared_weight)
    gathered = mix(part, shared_gain)
    return dot(gathered, output_weight).astype(jnp.bfloat16)


def solution(mesh):
    in_specs = (
        P("span", "tensor"),
        P("span"),
        P("tensor"),
        P("tensor"),
        P(None, "tensor"),
        P(None, "tensor"),
        P(None, "tensor"),
        P(None, None, "tensor"),
        P("tensor"),
        P("tensor", None),
        P(),
        P(None, "tensor"),
    )
    return jax.shard_map(shards, mesh=mesh, in_specs=in_specs, out_specs=P("span", "tensor"), check_vma=False)
```

time: 2300 us -> 100 us (0.04); the launches traced: 2270 us -> 98.9 us
  local copies, waits for them, and re-layouts: 2060 us -> 1.58 us
  matrix products: 66.7 us -> 1.16 us
  other arithmetic: 48.6 us -> 1.12 us
  waiting for transfers between devices: 60.3 us -> 32.7 us
    pad x6 -> x0, local copies, waits for them, and re-layouts: 931 us -> none  [shards(): inclusive = lax.associative_scan(block_combine, elements)]
    slice x21 -> x0, local copies, waits for them, and re-layouts: 549 us -> none  [the longest x1 153 us: shards(): inclusive[2][:-1]]
    unnamed x81 -> x8, local copies, waits for them, and re-layouts: 518 us -> 0.78 us
    dot_general x7 -> x1, matrix products: 66.7 us -> 1.16 us  [dot(): return jnp.dot(a, b, preferred_element_type=jnp.float32)]
    add x20 -> x0, other arithmetic: 26.1 us -> none  [the longest x11 18 us: shards(): inclusive = lax.associative_scan(block_combine, elements)]
  transfers between devices with their start and end apart: 7 -> 1, of which waited for: 7 -> 1; matrix products, arithmetic and copies ran while one was open for 0% -> 0% of each run, Pallas kernels for 0% -> 0%
where the time goes in v1:
time: 100 us; the launch traced here: 98.9 us
  blocking collectives  32.9 us (33%)
  waiting for transfers between devices  32.7 us (33%)
  Pallas kernels  16 us (16%)
  between operations  13.4 us (13%)
  local copies, waits for them, and re-layouts  1.58 us (2%)
  matrix products  1.16 us (1%)
  other arithmetic  1.12 us (1%)
    reduce_scatter x1, waiting for transfers between devices, mix(): lax.psum_scatter(part, 'tensor', scatter_dimension=0, tiled=True)  32.7 us
    all_gather x1, blocking collectives, mix(): return lax.all_gather(normed, 'tensor', axis=0, tiled=True)  18.5 us
    all_gather x2, blocking collectives, span_gather(): return lax.all_gather(values, 'span', axis=0)  14.4 us
    pallas_call x1, Pallas kernels, full_scan(): pl.pallas_call(full_kernel, out_shape=jax.ShapeDtypeStruct((length, weigh...  8.32 us
    pallas_call x1, Pallas kernels, local_scan(): pl.pallas_call(local_kernel, out_shape=(jax.ShapeDtypeStruct((length, cha...  5.75 us
  transfers between devices with their start and end apart: 1, of which 1 were waited for; matrix products, arithmetic and copies ran while one was open for 0% of the time, Pallas kernels for 0%

profile of v1, /device:TPU:7, one launch (start us, length us, event | category | flops | bytes accessed | tf_op | source)
XLA Modules:
  0.0 98.9 jit_solution(10762780960990411667)
XLA Ops:
  6.5 0.0 copy-start
  6.5 0.0 copy-start.2
  6.5 0.0 reduce-scatter.2.cloned.1.call-start
  6.5 0.8 copy-done.2
  7.3 0.8 copy.13.retain_ref
  8.1 1.9 %span_stats.1 = f32[8,512]{1,0:T(8,128)} custom-call(bf16[256,512]{1,0:T(8,128)(2,1)} %tokens_ref.3, f32[256,1]{1,0:T(8,128)} %copy.13.retain_ref), custom_call_target="tpu_custom_call" | custom-call | tf_op jit(solution)/shard_map/span_stats/pallas_call | solution.py:55
  10.0 7.2 %all-gather = f32[32,512]{1,0:T(8,128)} all-gather(f32[8,512]{1,0:T(8,128)} %span_stats.1), channel_id=2, replica_groups=mesh['span'=4,'tensor'=8] {'span'}, dimensions={0}, use_global_device_ids=true | all-gather | bytes 81920 | tf_op jit(solution)/shard_map/all_gather | solution.py:187
  17.2 5.7 %local_scan.1 = (f32[256,512]{1,0:T(8,128)}, bf16[32,512]{1,0:T(8,128)(2,1)}) custom-call(bf16[256,512]{1,0:T(8,128)(2,1)} %tokens_ref.3, f32[4,8,512]{2,1,0:T(8,128)} %bitcast.8, f32[256]{0:T(256)} %retain_ref.3, f32[1,512]{1,0:T(1,128)} %bitcast.12, f32[1,512]{1,0:T(1,128)} %bitcast.13, f32[16,512]{1,0:T(8,128)} %rate_ref.3, f32[16,512]{1,0:T(8,128)} %angle_ref.3), custom_call_target="tpu_custom_call" | custom-call | tf_op jit(solution)/shard_map/local_scan/pallas_call | solution.py:115
  22.9 7.2 %all-gather.1 = bf16[128,512]{1,0:T(8,128)(2,1)} all-gather(bf16[32,512]{1,0:T(8,128)(2,1)} %get-tuple-element.8), channel_id=3, replica_groups=mesh['span'=4,'tensor'=8] {'span'}, dimensions={0}, use_global_device_ids=true | all-gather | bytes 163840 | tf_op jit(solution)/shard_map/all_gather | solution.py:187
  30.2 8.3 %full_scan.1 = bf16[256,1024]{1,0:T(8,128)(2,1)} custom-call(f32[256,512]{1,0:T(8,128)} %get-tuple-element.7.normed_ref, bf16[4,32,512]{2,1,0:T(8,128)(2,1)} %bitcast.10, f32[4,8,512]{2,1,0:T(8,128)} %bitcast.9, f32[256]{0:T(256)} %retain_ref.3, f32[16,512]{1,0:T(8,128)} %rate_ref.3, f32[16,512]{1,0:T(8,128)} %angle_ref.3, f32[16,512]{1,0:T(8,128)} %input_ref.1, ...), custom_call_target="tpu_custom_call" | custom-call | tf_op jit(solution)/shard_map/full_scan/pallas_call | solution.py:176
  38.5 0.0 copy-start.3
  38.5 0.0 reduce-scatter.2.cloned.1.call-update
  38.5 32.7 %reduce-scatter.2.cloned.1.call-done = bf16[32,1024]{1,0:T(8,128)(2,1)} async-done(((bf16[256,1024]{1,0:T(8,128)(2,1)}), bf16[32,1024]{1,0:T(8,128)(2,1)}) %reduce-scatter.2.cloned.1.call-update) | async-done | bytes 65552 | tf_op jit(solution)/shard_map/reduce_scatter | solution.py:191
  71.2 0.0 copy-start.1
  71.2 1.0 %fusion = f32[32]{0:T(128)S(1)} fusion(bf16[32,1024]{1,0:T(8,128)(2,1)} %reduce-scatter.2.cloned.1.call-done), kind=kLoop, calls=%fused_computation.3 | loop fusion | flops 98272 | bytes 65664 | tf_op jit(solution)/shard_map/reduce_sum | solution.py:192
  72.3 0.0 copy-done.3
  72.3 0.0 copy-done.1
  72.3 0.1 fusion.2
  72.4 18.5 %all_gather.19 = bf16[256,1024]{1,0:T(8,128)(2,1)S(1)} all-gather(bf16[32,1024]{1,0:T(8,128)(2,1)S(1)} %fusion.2), channel_id=1, replica_groups=mesh['span'=4,'tensor'=8] {'tensor'}, dimensions={0}, use_global_device_ids=true | all-gather | bytes 589824 | tf_op jit(solution)/shard_map/all_gather | solution.py:194
  90.9 0.0 copy-done
  90.9 1.2 %convolution_convert_fusion = bf16[256,512]{1,0:T(8,128)(2,1)} fusion(bf16[256,1024]{1,0:T(8,128)(2,1)S(1)} %all_gather.19, bf16[1024,512]{1,0:T(8,128)(2,1)S(1)} %copy-done), kind=kOutput, calls=%fused_computation | convolution fusion | flops 268566528 | bytes 1835008 | tf_op jit(solution)/shard_map/dot_general | solution.py:20
  (1 shorter events, 0.0 us)
Async XLA Ops:
  6.5 84.3 %copy-start = (bf16[1024,512]{1,0:T(8,128)(2,1)S(1)}, bf16[1024,512]{1,0:T(8,128)(2,1)}, u32[]{:S(2)}) copy-start(bf16[1024,512]{1,0:T(8,128)(2,1)} %param.23) | copy-start | bytes 3145732
  6.5 0.8 copy-start.2
  6.5 64.7 %reduce-scatter.2.cloned.1.call-start = ((), (), s32[]{:S(2)}) async-start(), calls=%async_computation.1 | async-start | bytes 589824 | tf_op jit(solution)/shard_map/reduce_scatter | solution.py:191
  38.5 33.8 %copy-start.3 = (f32[1024]{0:T(1024)S(1)}, f32[1024]{0:T(1024)}, u32[]{:S(2)}) copy-start(f32[1024]{0:T(1024)} %param.22) | copy-start | bytes 12292
  71.2 1.1 %copy-start.1 = (bf16[32,1024]{1,0:T(8,128)(2,1)S(1)}, bf16[32,1024]{1,0:T(8,128)(2,1)}, u32[]{:S(2)}) copy-start(bf16[32,1024]{1,0:T(8,128)(2,1)} %reduce-scatter.2.cloned.1.call-done) | copy-start | bytes 196612
Sparse Core Ops, SparseCore 0:
  38.6 32.5 reduce-scatter.1

commit v2 on v1

--- a/solution.py
+++ b/solution.py
@@ -9,9 +9,11 @@
 
 GROUP = 64
 STEPS = 8
+KEPT = 16
 NORM_EPS = 1e-05
 SCALE_EPS = 1e-06
 
+MESH = pl.DeviceIdType.MESH
 VMEM = pl.BlockSpec(memory_space=pltpu.VMEM)
 SMEM = pl.BlockSpec(memory_space=pltpu.SMEM)
 
@@ -35,30 +37,92 @@
     return (row == column).astype(jnp.bfloat16)
 
 
-def stats_kernel(tokens_ref, retain_ref, stats_ref):
+def greet(axis, peers):
+    barrier = pltpu.get_barrier_semaphore()
+    for peer in peers:
+        pl.semaphore_signal(barrier, inc=1, device_id={axis: peer}, device_id_type=MESH)
+    pl.semaphore_wait(barrier, len(peers))
+
+
+def spread_copies(source, landing, send_sem, recv_sem, count):
+    me = lax.axis_index("span")
+    copies = []
+    for step in range(1, count):
+        copy = pltpu.make_async_remote_copy(
+            src_ref=source,
+            dst_ref=landing.at[me],
+            send_sem=send_sem.at[step - 1],
+            recv_sem=recv_sem.at[step - 1],
+            device_id={"span": lax.rem(me + step, count)},
+            device_id_type=MESH,
+        )
+        copies.append(copy)
+    return copies
+
+
+def span_peers(count):
+    me = lax.axis_index("span")
+    return [lax.rem(me + step, count) for step in range(1, count)]
+
+
+def stats_kernel(count, tokens_ref, stats_ref, own_ref, send_sem, recv_sem):
     length, channels = tokens_ref.shape
+    me = lax.axis_index("span")
     values = tokens_ref[...].astype(jnp.float32)
     total = jnp.sum(values, axis=0, keepdims=True)
     squares = jnp.sum(values * values, axis=0, keepdims=True)
     rows = jnp.concatenate([total, squares, jnp.zeros((6, channels), jnp.float32)], axis=0)
     ones = group_ones(channels)
-    grouped = sum(dot(piece, ones) for piece in pieces(rows, 3))
-    kept = retain_ref[...]
-    while kept.shape[0] > 1:
-        half = kept.shape[0] // 2
-        kept = kept[:half] * kept[half:]
-    row = lax.broadcasted_iota(jnp.int32, (8, channels), 0)
-    stats_ref[...] = jnp.where(row == 2, jnp.broadcast_to(kept, (8, channels)), grouped)
-
-
-def span_stats(tokens, retain):
+    own_ref[...] = sum(dot(piece, ones) for piece in pieces(rows, 3))
+    greet("span", span_peers(count))
+    copies = spread_copies(own_ref, stats_ref, send_sem, recv_sem, count)
+    for copy in copies:
+        copy.start()
+    stats_ref[me] = own_ref[...]
+    for copy in copies:
+        copy.wait()
+
+
+def span_stats(tokens):
+    count = lax.axis_size("span")
+    channels = tokens.shape[1]
     return pl.pallas_call(
-        stats_kernel,
-        out_shape=jax.ShapeDtypeStruct((8, tokens.shape[1]), jnp.float32),
-        in_specs=[VMEM, VMEM],
+        functools.partial(stats_kernel, count),
+        out_shape=jax.ShapeDtypeStruct((count, 8, channels), jnp.float32),
+        in_specs=[VMEM],
         out_specs=VMEM,
+        scratch_shapes=[
+            pltpu.VMEM((8, channels), jnp.float32),
+            pltpu.SemaphoreType.DMA((count - 1,)),
+            pltpu.SemaphoreType.DMA((count - 1,)),
+        ],
+        compiler_params=pltpu.CompilerParams(collective_id=0, has_side_effects=True),
         name="span_stats",
-    )(tokens, retain.reshape(-1, 1))
+    )(tokens)
+
+
+def gather_kernel(count, own_ref, all_ref, send_sem, recv_sem):
+    me = lax.axis_index("span")
+    greet("span", span_peers(count))
+    copies = spread_copies(own_ref, all_ref, send_sem, recv_sem, count)
+    for copy in copies:
+        copy.start()
+    all_ref[me] = own_ref[...]
+    for copy in copies:
+        copy.wait()
+
+
+def span_gather(values):
+    count = lax.axis_size("span")
+    return pl.pallas_call(
+        functools.partial(gather_kernel, count),
+        out_shape=jax.ShapeDtypeStruct((count,) + values.shape, values.dtype),
+        in_specs=[VMEM],
+        out_specs=VMEM,
+        scratch_shapes=[pltpu.SemaphoreType.DMA((count - 1,)), pltpu.SemaphoreType.DMA((count - 1,))],
+        compiler_params=pltpu.CompilerParams(collective_id=1, has_side_effects=True),
+        name="span_gather",
+    )(values)
 
 
 def local_kernel(tokens_ref, stats_ref, retain_ref, gain_ref, bias_ref, rate_ref, angle_ref, normed_ref, state_ref):
@@ -93,21 +157,26 @@
         turn_im = size * jnp.sin(angle_ref[:, lanes])
 
         def steps(block, carried):
-            re, im = carried
+            re, im, kept = carried
             first = pl.multiple_of(block * STEPS, STEPS)
             for step in range(STEPS):
                 entry = normed_ref[pl.ds(first + step, 1), lanes]
                 keep = retain_ref[first + step]
+                kept = kept * keep
                 re, im = (
                     (turn_re * re - turn_im * im) * keep + entry,
                     (turn_re * im + turn_im * re) * keep,
                 )
-            return re, im
+            return re, im, kept
 
         zero = jnp.zeros((ndim, width), jnp.float32)
-        re, im = lax.fori_loop(0, length // STEPS, steps, (zero, zero))
+        re, im, kept = lax.fori_loop(0, length // STEPS, steps, (zero, zero, jnp.float32(1.0)))
         state_ref[0:ndim, lanes] = re.astype(state_ref.dtype)
-        state_ref[ndim:, lanes] = im.astype(state_ref.dtype)
+        state_ref[ndim : 2 * ndim, lanes] = im.astype(state_ref.dtype)
+        high, middle, low = pieces(jnp.full((KEPT, width), kept, jnp.float32), 3)
+        row = lax.broadcasted_iota(jnp.int32, (KEPT, width), 0)
+        rest = jnp.where(row == 1, middle.astype(jnp.float32), low.astype(jnp.float32))
+        state_ref[2 * ndim :, lanes] = jnp.where(row == 0, high.astype(jnp.float32), rest).astype(state_ref.dtype)
 
 
 def local_scan(tokens, stats, retain, gain, bias, rate, angle):
@@ -116,7 +185,7 @@
         local_kernel,
         out_shape=(
             jax.ShapeDtypeStruct((length, channels), jnp.float32),
-            jax.ShapeDtypeStruct((2 * rate.shape[0], channels), jnp.bfloat16),
+            jax.ShapeDtypeStruct((2 * rate.shape[0] + KEPT, channels), jnp.bfloat16),
         ),
         in_specs=[VMEM, VMEM, SMEM, VMEM, VMEM, VMEM, VMEM],
         out_specs=(VMEM, VMEM),
@@ -124,7 +193,7 @@
     )(tokens, stats, retain, gain.reshape(1, -1), bias.reshape(1, -1), rate, angle)
 
 
-def full_kernel(normed_ref, states_ref, stats_ref, retain_ref, rate_ref, angle_ref, input_ref, output_ref, skip_ref, weight_ref, part_ref, ema_ref):
+def full_kernel(normed_ref, states_ref, retain_ref, rate_ref, angle_ref, input_ref, output_ref, skip_ref, weight_ref, part_ref, ema_ref):
     length, channels = normed_ref.shape
     ndim = rate_ref.shape[0]
     me = lax.axis_index("span")
@@ -144,9 +213,10 @@
         re = jnp.zeros((ndim, width), jnp.float32)
         im = jnp.zeros((ndim, width), jnp.float32)
         for other in range(states_ref.shape[0]):
-            keep = stats_ref[other, 2:3, lanes]
+            kept = states_ref[other, 2 * ndim :, lanes].astype(jnp.float32)
+            keep = kept[0:1] + kept[1:2] + kept[2:3]
             here_re = states_ref[other, 0:ndim, lanes].astype(jnp.float32)
-            here_im = states_ref[other, ndim:, lanes].astype(jnp.float32)
+            here_im = states_ref[other, ndim : 2 * ndim, lanes].astype(jnp.float32)
             next_re = (whole_re * re - whole_im * im) * keep + here_re
             next_im = (whole_re * im + whole_im * re) * keep + here_im
             re = jnp.where(other < me, next_re, re)
@@ -171,34 +241,112 @@
     part_ref[...] = dot(active, weight_ref[...]).astype(jnp.bfloat16)
 
 
-def full_scan(normed, states, stats, retain, rate, angle, source, output, skip, weight):
+def full_scan(normed, states, retain, rate, angle, source, output, skip, weight):
     length, channels = normed.shape
     return pl.pallas_call(
         full_kernel,
         out_shape=jax.ShapeDtypeStruct((length, weight.shape[1]), jnp.bfloat16),
-        in_specs=[VMEM, VMEM, VMEM, SMEM] + [VMEM] * 6,
+        in_specs=[VMEM, VMEM, SMEM] + [VMEM] * 6,
         out_specs=VMEM,
         scratch_shapes=[pltpu.VMEM((length, channels), jnp.float32)],
         name="full_scan",
-    )(normed, states, stats, retain, rate, angle, source, output, skip.reshape(1, -1), weight)
-
-
-def span_gather(values):
-    return lax.all_gather(values, "span", axis=0)
+    )(normed, states, retain, rate, angle, source, output, skip.reshape(1, -1), weight)
+
+
+def mix_kernel(chips, part_ref, gain_ref, out_ref, near_ref, sum_ref, far_ref, own_ref, pair_send, pair_recv, far_send, far_recv, out_send, out_recv, back_send, back_recv):
+    me = lax.axis_index("tensor")
+    core = lax.rem(me, 2)
+    chip = lax.div(me, 2)
+    partner = me + 1 - 2 * core
+    order = [lax.rem(chip + step, chips) for step in range(1, chips)] + [chip]
+    peers = [2 * place + core for place in order[:-1]]
+    greet("tensor", [partner] + peers)
+
+    def send(source, target, send_sem, recv_sem, device):
+        return pltpu.make_async_remote_copy(
+            src_ref=source,
+            dst_ref=target,
+            send_sem=send_sem,
+            recv_sem=recv_sem,
+            device_id={"tensor": device},
+            device_id_type=MESH,
+        )
+
+    pair = []
+    for slot, place in enumerate(order):
+        copy = send(part_ref.at[place, 1 - core], near_ref.at[slot], pair_send.at[slot], pair_recv.at[slot], partner)
+        copy.start()
+        pair.append(copy)
+    far = []
+    for slot, place in enumerate(order[:-1]):
+        pair[slot].wait_recv()
+        added = part_ref[place, core].astype(jnp.float32) + near_ref[slot].astype(jnp.float32)
+        sum_ref[slot] = added.astype(jnp.bfloat16)
+        copy = send(sum_ref.at[slot], far_ref.at[slot], far_send.at[slot], far_recv.at[slot], peers[slot])
+        copy.start()
+        far.append(copy)
+    pair[-1].wait_recv()
+    shared = part_ref[chip, core].astype(jnp.float32) + near_ref[chips - 1].astype(jnp.float32)
+    for slot in range(chips - 1):
+        far[slot].wait_recv()
+        shared = shared + far_ref[slot].astype(jnp.float32)
+    squares = jnp.mean(shared * shared, axis=1, keepdims=True)
+    own_ref[...] = (shared * lax.rsqrt(squares + SCALE_EPS) * gain_ref[...]).astype(jnp.bfloat16)
+    outward = []
+    for slot in range(chips - 1):
+        copy = send(own_ref, out_ref.at[chip, core], out_send.at[slot], out_recv.at[slot], peers[slot])
+        copy.start()
+        outward.append(copy)
+    back = [send(own_ref, out_ref.at[chip, core], back_send.at[chips - 1], back_recv.at[chips - 1], partner)]
+    back[0].start()
+    out_ref[chip, core] = own_ref[...]
+    for slot in range(chips - 1):
+        origin = lax.rem(chip + chips - 1 - slot, chips)
+        outward[slot].wait_recv()
+        block = out_ref.at[origin, core]
+        copy = send(block, block, back_send.at[slot], back_recv.at[slot], partner)
+        copy.start()
+        back.append(copy)
+    for copy in back:
+        copy.wait()
+    for copy in pair + far + outward:
+        copy.wait_send()
 
 
 def mix(part, gain):
-    shared = lax.psum_scatter(part, "tensor", scatter_dimension=0, tiled=True).astype(jnp.float32)
-    squares = jnp.mean(shared * shared, axis=1, keepdims=True)
-    normed = (shared * lax.rsqrt(squares + SCALE_EPS) * gain[None]).astype(jnp.bfloat16)
-    return lax.all_gather(normed, "tensor", axis=0, tiled=True)
+    chips = lax.axis_size("tensor") // 2
+    rows, columns = part.shape[0] // (2 * chips), part.shape[1]
+    block = (rows, columns)
+    gathered = pl.pallas_call(
+        functools.partial(mix_kernel, chips),
+        out_shape=jax.ShapeDtypeStruct((chips, 2) + block, jnp.bfloat16),
+        in_specs=[VMEM, VMEM],
+        out_specs=VMEM,
+        scratch_shapes=[
+            pltpu.VMEM((chips,) + block, jnp.bfloat16),
+            pltpu.VMEM((chips - 1,) + block, jnp.bfloat16),
+            pltpu.VMEM((chips - 1,) + block, jnp.bfloat16),
+            pltpu.VMEM(block, jnp.bfloat16),
+            pltpu.SemaphoreType.DMA((chips,)),
+            pltpu.SemaphoreType.DMA((chips,)),
+            pltpu.SemaphoreType.DMA((chips - 1,)),
+            pltpu.SemaphoreType.DMA((chips - 1,)),
+            pltpu.SemaphoreType.DMA((chips - 1,)),
+            pltpu.SemaphoreType.DMA((chips - 1,)),
+            pltpu.SemaphoreType.DMA((chips,)),
+            pltpu.SemaphoreType.DMA((chips,)),
+        ],
+        compiler_params=pltpu.CompilerParams(collective_id=2, has_side_effects=True),
+        name="mix",
+    )(part.reshape((chips, 2) + block), gain.reshape(1, -1))
+    return gathered.reshape(part.shape)
 
 
 def shards(tokens, retain, norm_gain, norm_bias, decay_rate, ema_angle, ema_input, ema_output, ema_skip, shared_weight, shared_gain, output_weight):
-    stats = span_gather(span_stats(tokens, retain))
+    stats = span_stats(tokens)
     normed, state = local_scan(tokens, stats, retain, norm_gain, norm_bias, decay_rate, ema_angle)
     states = span_gather(state)
-    part = full_scan(normed, states, stats, retain, decay_rate, ema_angle, ema_input, ema_output, ema_skip, shared_weight)
+    part = full_scan(normed, states, retain, decay_rate, ema_angle, ema_input, ema_output, ema_skip, shared_weight)
     gathered = mix(part, shared_gain)
     return dot(gathered, output_weight).astype(jnp.bfloat16)
 

time: 100 us -> 51.6 us (0.52)
  the two profiles are of different devices: /device:TPU:7 before, /device:TPU:0 now
where the time goes in v2:
time: 51.6 us; the launch traced here: 51.3 us
  Pallas kernels  49.1 us (95%)
  matrix products  2.18 us (4%)
    pallas_call x1, Pallas kernels, mix(): pl.pallas_call(functools.partial(mix_kernel, chips), out_shape=jax.ShapeD...  19.5 us
    pallas_call x1, Pallas kernels, span_stats(): pl.pallas_call(functools.partial(stats_kernel, count), out_shape=jax.Shap...  8.42 us
    pallas_call x1, Pallas kernels, full_scan(): pl.pallas_call(full_kernel, out_shape=jax.ShapeDtypeStruct((length, weigh...  8.36 us
    pallas_call x1, Pallas kernels, span_gather(): pl.pallas_call(functools.partial(gather_kernel, count), out_shape=jax.Sha...  7.05 us
    pallas_call x1, Pallas kernels, local_scan(): pl.pallas_call(local_kernel, out_shape=(jax.ShapeDtypeStruct((length, cha...  5.75 us
    dot_general x1, matrix products, dot(): return jnp.dot(a, b, preferred_element_type=jnp.float32)  2.18 us

profile of v2, /device:TPU:0, one launch (start us, length us, event | category | flops | bytes accessed | tf_op | source)
XLA Modules:
  0.0 51.3 jit_solution(4324556208419993543)
XLA Ops:
  0.0 0.0 copy-start
  0.0 8.4 %span_stats.1.stats_ref = f32[4,8,512]{2,1,0:T(8,128)} custom-call(bf16[256,512]{1,0:T(8,128)(2,1)} %tokens_ref.3), custom_call_target="tpu_custom_call" | custom-call | tf_op jit(solution)/shard_map/span_stats/pallas_call | solution.py:89
  8.4 5.8 %local_scan.1 = (f32[256,512]{1,0:T(8,128)}, bf16[48,512]{1,0:T(8,128)(2,1)}) custom-call(bf16[256,512]{1,0:T(8,128)(2,1)} %tokens_ref.3, f32[4,8,512]{2,1,0:T(8,128)} %span_stats.1.stats_ref, f32[256]{0:T(256)} %retain_ref.3, f32[1,512]{1,0:T(1,128)} %bitcast.11, f32[1,512]{1,0:T(1,128)} %bitcast.12, f32[16,512]{1,0:T(8,128)} %rate_ref.3, f32[16,512]{1,0:T(8,128)} %angle_ref.3), custom_call_target="tpu_custom_call" | custom-call | tf_op jit(solution)/shard_map/local_scan/pallas_call | solution.py:184
  14.2 7.1 %span_gather.1.states_ref = bf16[4,48,512]{2,1,0:T(8,128)(2,1)} custom-call(bf16[48,512]{1,0:T(8,128)(2,1)} %get-tuple-element.8.own_ref), custom_call_target="tpu_custom_call" | custom-call | tf_op jit(solution)/shard_map/span_gather/pallas_call | solution.py:117
  21.2 8.4 %full_scan.1 = bf16[256,1024]{1,0:T(8,128)(2,1)} custom-call(f32[256,512]{1,0:T(8,128)} %get-tuple-element.7.normed_ref, bf16[4,48,512]{2,1,0:T(8,128)(2,1)} %span_gather.1.states_ref, f32[256]{0:T(256)} %retain_ref.3, f32[16,512]{1,0:T(8,128)} %rate_ref.3, f32[16,512]{1,0:T(8,128)} %angle_ref.3, f32[16,512]{1,0:T(8,128)} %input_ref.1, ...), custom_call_target="tpu_custom_call" | custom-call | tf_op jit(solution)/shard_map/full_scan/pallas_call | solution.py:246
  29.6 19.5 %mix.1 = bf16[4,2,32,1024]{3,2,1,0:T(8,128)(2,1)} custom-call(bf16[4,2,32,1024]{3,2,1,0:T(8,128)(2,1)} %bitcast.9, f32[1,1024]{1,0:T(1,128)} %bitcast.10), custom_call_target="tpu_custom_call" | custom-call | tf_op jit(solution)/shard_map/mix/pallas_call | solution.py:320
  49.1 0.0 copy-done
  49.2 2.2 %convolution_convert_fusion = bf16[256,512]{1,0:T(8,128)(2,1)} fusion(bf16[256,1024]{1,0:T(8,128)(2,1)} %bitcast.8, bf16[1024,512]{1,0:T(8,128)(2,1)S(1)} %copy-done), kind=kOutput, calls=%fused_computation | convolution fusion | flops 268566528 | bytes 1835008 | tf_op jit(solution)/shard_map/dot_general | solution.py:22
Async XLA Ops:
  0.0 49.1 %copy-start = (bf16[1024,512]{1,0:T(8,128)(2,1)S(1)}, bf16[1024,512]{1,0:T(8,128)(2,1)}, u32[]{:S(2)}) copy-start(bf16[1024,512]{1,0:T(8,128)(2,1)} %param.23) | copy-start | bytes 3145732

commit v3 on v1

v3 whole, which is shorter than its diff:
```python
import functools

import jax
import jax.numpy as jnp
from jax import lax
from jax.experimental import pallas as pl
from jax.experimental.pallas import tpu as pltpu
from jax.sharding import PartitionSpec as P

GROUP = 64
STEPS = 8
LANES = 128
NORM_EPS = 1e-05
SCALE_EPS = 1e-06

MESH = pl.DeviceIdType.MESH
VMEM = pl.BlockSpec(memory_space=pltpu.VMEM)


def dot(a, b):
    return jnp.dot(a, b, preferred_element_type=jnp.float32)


def pieces(values, count):
    out = []
    for _ in range(count):
        piece = values.astype(jnp.bfloat16)
        out.append(piece)
        values = values - piece.astype(jnp.float32)
    return out


def group_ones(channels):
    row = lax.broadcasted_iota(jnp.int32, (channels, channels), 0) // GROUP
    column = lax.broadcasted_iota(jnp.int32, (channels, channels), 1) // GROUP
    return (row == column).astype(jnp.bfloat16)


def remote(source, target, send_sem, recv_sem, axis, device):
    return pltpu.make_async_remote_copy(
        src_ref=source,
        dst_ref=target,
        send_sem=send_sem,
        recv_sem=recv_sem,
        device_id={axis: device},
        device_id_type=MESH,
    )


def to_later(count, pairs, send_sem, recv_sem):
    me = lax.axis_index("span")
    for step in range(1, count):

        @pl.when(me + step < count)
        def _():
            for item, (source, landing) in enumerate(pairs):
                remote(source, landing.at[me], send_sem.at[item, step - 1], recv_sem.at[item, step - 1], "span", me + step).start()


def from_earlier(count, pairs, send_sem, recv_sem):
    me = lax.axis_index("span")
    for step in range(1, count):

        @pl.when(me >= step)
        def _():
            for item, (source, landing) in enumerate(pairs):
                remote(source, landing.at[me], send_sem.at[item, step - 1], recv_sem.at[item, step - 1], "span", me - step).wait_recv()

        @pl.when(me + step < count)
        def _():
            for item, (source, landing) in enumerate(pairs):
                remote(source, landing.at[me], send_sem.at[item, step - 1], recv_sem.at[item, step - 1], "span", me + step).wait_send()


def wide(column, width):
    return jnp.concatenate([column] * (width // LANES), axis=1)


def lanes_of(channels, width):
    return [slice(start, start + width) for start in range(0, channels, width)]


def layer_kernel(
    count,
    chips,
    tokens_ref,
    retain_ref,
    norm_gain_ref,
    bias_ref,
    rate_ref,
    angle_ref,
    input_ref,
    output_ref,
    skip_ref,
    gain_ref,
    weight_hbm,
    mixer_hbm,
    out_ref,
    weight_ref,
    mixer_ref,
    total_ref,
    totals_ref,
    before_ref,
    normed_ref,
    scaled_ref,
    prefix_ref,
    power_ref,
    unit_ref,
    read_ref,
    start_ref,
    state_ref,
    states_ref,
    kept_ref,
    kepts_ref,
    ema_ref,
    part_ref,
    near_ref,
    sum_ref,
    far_ref,
    own_ref,
    all_ref,
    load_sem,
    total_send,
    total_recv,
    state_send,
    state_recv,
    pair_send,
    pair_recv,
    far_send,
    far_recv,
    out_send,
    out_recv,
    back_send,
    back_recv,
):
    length, channels = tokens_ref.shape
    ndim = rate_ref.shape[0]
    blocks = length // STEPS
    rows = part_ref.shape[2]
    span = lax.axis_index("span")
    me = lax.axis_index("tensor")
    core = lax.rem(me, 2)
    chip = lax.div(me, 2)
    partner = me + 1 - 2 * core
    order = [lax.rem(chip + step, chips) for step in range(1, chips)] + [chip]
    peers = [2 * place + core for place in order[:-1]]

    barrier = pltpu.get_barrier_semaphore()
    for step in range(1, count):
        pl.semaphore_signal(barrier, inc=1, device_id={"span": lax.rem(span + step, count)}, device_id_type=MESH)
    for peer in [partner] + peers:
        pl.semaphore_signal(barrier, inc=1, device_id={"tensor": peer}, device_id_type=MESH)
    loads = [
        pltpu.make_async_copy(weight_hbm, weight_ref, load_sem.at[0]),
        pltpu.make_async_copy(mixer_hbm, mixer_ref, load_sem.at[1]),
    ]
    for load in loads:
        load.start()

    tokens = tokens_ref[...]
    values = tokens.astype(jnp.float32)
    ones = group_ones(channels)
    total = jnp.sum(values, axis=0, keepdims=True)
    squares = jnp.sum(values * values, axis=0, keepdims=True)
    summed = jnp.concatenate([total, squares, jnp.zeros((6, channels), jnp.float32)], axis=0)
    total_ref[...] = sum(dot(piece, ones) for piece in pieces(summed, 3))
    pl.semaphore_wait(barrier, count - 1 + chips)
    stats_pairs = [(total_ref, totals_ref)]
    to_later(count, stats_pairs, total_send, total_recv)

    rate, angle = rate_ref[...], angle_ref[...]
    size = jnp.exp(-rate)
    turn_re = size * jnp.cos(angle)
    turn_im = size * jnp.sin(angle)
    weight = (1.0 - size) * input_ref[...]
    read_re = weight * output_ref[0]
    read_im = weight * output_ref[1]
    power_re, power_im = jnp.ones_like(rate), jnp.zeros_like(rate)
    lag_rows = []
    for lag in range(STEPS + 1):
        if lag < STEPS:
            lag_rows.append(jnp.sum(read_re * power_re - read_im * power_im, axis=0, keepdims=True))
        power_ref[0, lag] = power_re
        power_ref[1, lag] = power_im
        power_re, power_im = power_re * turn_re - power_im * turn_im, power_re * turn_im + power_im * turn_re
    unit_ref[0] = read_re * turn_re - read_im * turn_im
    unit_ref[1] = read_re * turn_im + read_im * turn_re
    step_row = lax.broadcasted_iota(jnp.int32, (STEPS, channels), 0)

    def table(part, carried):
        here = pl.ds(part, 1)
        re = jnp.broadcast_to(unit_ref[0, here, :], (STEPS, channels))
        im = jnp.broadcast_to(unit_ref[1, here, :], (STEPS, channels))
        for bit in (1, 2, 4):
            chosen = (step_row // bit) % 2 == 1
            by_re = jnp.where(chosen, jnp.broadcast_to(power_ref[0, bit, here, :], (STEPS, channels)), 1.0)
            by_im = jnp.where(chosen, jnp.broadcast_to(power_ref[1, bit, here, :], (STEPS, channels)), 0.0)
            re, im = re * by_re - im * by_im, re * by_im + im * by_re
        read_ref[0, part] = re
        read_ref[1, part] = im
        return carried

    lax.fori_loop(0, ndim, table, 0)

    sums = dot(tokens, ones)
    squares = sum(dot(piece, ones) for piece in pieces(values * values, 2))
    row = lax.broadcasted_iota(jnp.int32, (length, length), 0)
    column = lax.broadcasted_iota(jnp.int32, (length, length), 1)
    lower = (column <= row).astype(jnp.bfloat16)
    cum_sum = sum(dot(lower, piece) for piece in pieces(sums, 3))
    cum_sq = sum(dot(lower, piece) for piece in pieces(squares, 3))
    diagonal = jnp.where(row == column, jnp.broadcast_to(retain_ref[...], (length, length)), 0.0)
    keep = sum(dot(piece, jnp.ones((length, LANES), jnp.bfloat16)) for piece in pieces(diagonal, 3))
    place_in = lax.broadcasted_iota(jnp.int32, (length, LANES), 0) % STEPS
    prefix = keep
    suffix = jnp.where(place_in < STEPS - 1, pltpu.roll(keep, length - 1, 0), 1.0)
    for by in (1, 2, 4):
        prefix = jnp.where(place_in >= by, prefix * pltpu.roll(prefix, by, 0), prefix)
        suffix = jnp.where(place_in + by < STEPS, suffix * pltpu.roll(suffix, length - by, 0), suffix)
    prefix_ref[...] = prefix
    position = lax.broadcasted_iota(jnp.int32, (length, channels), 0)
    counts = ((span * length + position + 1) * GROUP).astype(jnp.float32)

    from_earlier(count, stats_pairs, total_send, total_recv)
    before_ref[...] = jnp.zeros((8, channels), jnp.float32)
    for other in range(count - 1):

        @pl.when(other < span)
        def _():
            before_ref[...] += totals_ref[other]

    average = (before_ref[0:1] + cum_sum) / counts
    spread = (before_ref[1:2] + cum_sq) / counts - average * average
    inverse = lax.rsqrt(spread + NORM_EPS)
    normed = (values - average) * inverse * norm_gain_ref[...] + bias_ref[...]
    normed_ref[...] = normed
    scaled_ref[...] = normed * wide(suffix, channels)

    width = min(256, channels)
    for lanes in lanes_of(channels, width):
        whole_re, whole_im = power_ref[0, STEPS, :, lanes], power_ref[1, STEPS, :, lanes]

        def enter(block, carried):
            re, im, kept = carried
            start_ref[0, block, :, lanes] = re
            start_ref[1, block, :, lanes] = im
            first = pl.multiple_of(block * STEPS, STEPS)
            factor = wide(prefix_ref[pl.ds(first + STEPS - 1, 1), :], width)
            next_re = (whole_re * re - whole_im * im) * factor
            next_im = (whole_re * im + whole_im * re) * factor
            for step in range(STEPS):
                entry = scaled_ref[pl.ds(first + step, 1), lanes]
                lag = STEPS - 1 - step
                if lag:
                    next_re = next_re + power_ref[0, lag, :, lanes] * entry
                    next_im = next_im + power_ref[1, lag, :, lanes] * entry
                else:
                    next_re = next_re + entry
            return next_re, next_im, kept * factor

        zero = jnp.zeros((ndim, width), jnp.float32)
        re, im, kept = lax.fori_loop(0, blocks, enter, (zero, zero, jnp.ones((1, width), jnp.float32)))
        state_ref[0:ndim, lanes] = re.astype(state_ref.dtype)
        state_ref[ndim : 2 * ndim, lanes] = im.astype(state_ref.dtype)
    kept_ref[...] = jnp.broadcast_to(kept[:, :LANES], (8, LANES))
    state_pairs = [(state_ref, states_ref), (kept_ref, kepts_ref)]
    to_later(count, state_pairs, state_send, state_recv)

    for lanes in lanes_of(channels, LANES):
        reach = jnp.where(place_in >= 0, 1.0, 0.0)
        here = normed_ref[:, lanes]
        within = here * lag_rows[0][:, lanes]
        for lag in range(1, STEPS):
            reach = jnp.where(place_in >= lag, reach * (pltpu.roll(keep, lag - 1, 0) if lag > 1 else keep), 0.0)
            within = within + pltpu.roll(here, lag, 0) * (lag_rows[lag][:, lanes] * reach)
        ema_ref[:, lanes] = within + skip_ref[:, lanes] * here

    from_earlier(count, state_pairs, state_send, state_recv)
    whole = jnp.exp(-rate * length)
    unit_ref[0] = whole * jnp.cos(angle * length)
    unit_ref[1] = whole * jnp.sin(angle * length)
    power_ref[0, 0] = jnp.zeros_like(rate)
    power_ref[1, 0] = jnp.zeros_like(rate)
    for other in range(count - 1):

        @pl.when(other < span)
        def _():
            kept = wide(kepts_ref[other, 0:1, :], channels)
            re, im = power_ref[0, 0], power_ref[1, 0]
            by_re, by_im = unit_ref[0], unit_ref[1]
            power_ref[0, 0] = (by_re * re - by_im * im) * kept + states_ref[other, 0:ndim].astype(jnp.float32)
            power_ref[1, 0] = (by_re * im + by_im * re) * kept + states_ref[other, ndim : 2 * ndim].astype(jnp.float32)

    for lanes in lanes_of(channels, width):
        whole_re, whole_im = power_ref[0, STEPS, :, lanes], power_ref[1, STEPS, :, lanes]

        def arrive(block, carried):
            re, im = carried
            start_ref[0, block, :, lanes] += re
            start_ref[1, block, :, lanes] += im
            factor = wide(prefix_ref[pl.ds(block * STEPS + STEPS - 1, 1), :], width)
            return (whole_re * re - whole_im * im) * factor, (whole_re * im + whole_im * re) * factor

        lax.fori_loop(0, blocks, arrive, (power_ref[0, 0, :, lanes], power_ref[1, 0, :, lanes]))

        def leave(block, carried):
            first = pl.multiple_of(block * STEPS, STEPS)
            parts = [jnp.zeros((STEPS, width), jnp.float32) for _ in range(4)]
            for part in range(ndim):
                here = pl.ds(part, 1)
                slot = 2 * (part % 2)
                parts[slot] = parts[slot] + read_ref[0, part, :, lanes] * start_ref[0, block, here, lanes]
                parts[slot + 1] = parts[slot + 1] + read_ref[1, part, :, lanes] * start_ref[1, block, here, lanes]
            read = (parts[0] - parts[1]) + (parts[2] - parts[3])
            ema_ref[pl.ds(first, STEPS), lanes] += read * wide(prefix_ref[pl.ds(first, STEPS), :], width)
            return carried

        lax.fori_loop(0, blocks, leave, 0)

    ema = ema_ref[...]
    active = (ema / (1.0 + jnp.exp(-ema))).astype(jnp.bfloat16)
    for load in loads:
        load.wait()
    product = dot(active, weight_ref[...]).astype(jnp.bfloat16)
    part_ref[...] = product.reshape(part_ref.shape)

    pair = []
    for slot, place in enumerate(order):
        copy = remote(part_ref.at[place, 1 - core], near_ref.at[slot], pair_send.at[slot], pair_recv.at[slot], "tensor", partner)
        copy.start()
        pair.append(copy)
    far = []
    for slot, place in enumerate(order[:-1]):
        pair[slot].wait_recv()
        added = part_ref[place, core].astype(jnp.float32) + near_ref[slot].astype(jnp.float32)
        sum_ref[slot] = added.astype(jnp.bfloat16)
        copy = remote(sum_ref.at[slot], far_ref.at[slot], far_send.at[slot], far_recv.at[slot], "tensor", peers[slot])
        copy.start()
        far.append(copy)
    pair[-1].wait_recv()
    shared = part_ref[chip, core].astype(jnp.float32) + near_ref[chips - 1].astype(jnp.float32)
    for slot in range(chips - 1):
        far[slot].wait_recv()
        shared = shared + far_ref[slot].astype(jnp.float32)
    squares = jnp.mean(shared * shared, axis=1, keepdims=True)
    own_ref[...] = (shared * lax.rsqrt(squares + SCALE_EPS) * gain_ref[...]).astype(jnp.bfloat16)
    outward = []
    for slot in range(chips - 1):
        copy = remote(own_ref, all_ref.at[chip, core], out_send.at[slot], out_recv.at[slot], "tensor", peers[slot])
        copy.start()
        outward.append(copy)
    home = remote(own_ref, all_ref.at[chip, core], back_send.at[chips - 1], back_recv.at[chips - 1], "tensor", partner)
    home.start()
    all_ref[chip, core] = own_ref[...]
    columns = all_ref.shape[3]

    def finish(place):
        gathered = all_ref[place].reshape(2 * rows, columns)
        out_ref[place] = dot(gathered, mixer_ref[...]).astype(jnp.bfloat16)

    home.wait_recv()
    finish(chip)
    back = []
    for slot in range(chips - 1):
        origin = lax.rem(chip + chips - 1 - slot, chips)
        outward[slot].wait_recv()
        block = all_ref.at[origin, core]
        copy = remote(block, block, back_send.at[slot], back_recv.at[slot], "tensor", partner)
        copy.start()
        back.append(copy)
        if slot:
            back[slot - 1].wait_recv()
            finish(lax.rem(chip + chips - slot, chips))
    back[-1].wait_recv()
    finish(lax.rem(chip + 1, chips))
    for copy in pair + far + outward + back + [home]:
        copy.wait_send()


def layer(tokens, retain, norm_gain, norm_bias, rate, angle, source, output, skip, weight, gain, mixer):
    length, channels = tokens.shape
    ndim = rate.shape[0]
    blocks = length // STEPS
    count = lax.axis_size("span")
    chips = lax.axis_size("tensor") // 2
    rows, columns = length // (2 * chips), weight.shape[1]
    block = (rows, columns)
    f32, bf16 = jnp.float32, jnp.bfloat16
    sems = pltpu.SemaphoreType.DMA
    hbm = pl.BlockSpec(memory_space=pltpu.HBM)
    out = pl.pallas_call(
        functools.partial(layer_kernel, count, chips),
        out_shape=jax.ShapeDtypeStruct((chips, 2 * rows, mixer.shape[1]), bf16),
        in_specs=[VMEM] * 10 + [hbm, hbm],
        out_specs=VMEM,
        scratch_shapes=[
            pltpu.VMEM(weight.shape, bf16),
            pltpu.VMEM(mixer.shape, bf16),
            pltpu.VMEM((8, channels), f32),
            pltpu.VMEM((count, 8, channels), f32),
            pltpu.VMEM((8, channels), f32),
            pltpu.VMEM((length, channels), f32),
            pltpu.VMEM((length, channels), f32),
            pltpu.VMEM((length, LANES), f32),
            pltpu.VMEM((2, STEPS + 1, ndim, channels), f32),
            pltpu.VMEM((2, ndim, channels), f32),
            pltpu.VMEM((2, ndim, STEPS, channels), f32),
            pltpu.VMEM((2, blocks, ndim, channels), f32),
            pltpu.VMEM((2 * ndim, channels), bf16),
            pltpu.VMEM((count, 2 * ndim, channels), bf16),
            pltpu.VMEM((8, LANES), f32),
            pltpu.VMEM((count, 8, LANES), f32),
            pltpu.VMEM((length, channels), f32),
            pltpu.VMEM((chips, 2) + block, bf16),
            pltpu.VMEM((chips,) + block, bf16),
            pltpu.VMEM((chips - 1,) + block, bf16),
            pltpu.VMEM((chips - 1,) + block, bf16),
            pltpu.VMEM(block, bf16),
            pltpu.VMEM((chips, 2) + block, bf16),
            sems((2,)),
            sems((1, count - 1)),
            sems((1, count - 1)),
            sems((2, count - 1)),
            sems((2, count - 1)),
            sems((chips,)),
            sems((chips,)),
            sems((chips - 1,)),
            sems((chips - 1,)),
            sems((chips - 1,)),
            sems((chips - 1,)),
            sems((chips,)),
            sems((chips,)),
        ],
        compiler_params=pltpu.CompilerParams(collective_id=0, has_side_effects=True, vmem_limit_bytes=40 << 20),
        name="layer",
    )(
        tokens,
        retain.reshape(1, -1),
        norm_gain.reshape(1, -1),
        norm_bias.reshape(1, -1),
        rate,
        angle,
        source,
        output,
        skip.reshape(1, -1),
        gain.reshape(1, -1),
        weight,
        mixer,
    )
    return out.reshape(length, mixer.shape[1])


def solution(mesh):
    in_specs = (
        P("span", "tensor"),
        P("span"),
        P("tensor"),
        P("tensor"),
        P(None, "tensor"),
        P(None, "tensor"),
        P(None, "tensor"),
        P(None, None, "tensor"),
        P("tensor"),
        P("tensor", None),
        P(),
        P(None, "tensor"),
    )
    return jax.shard_map(layer, mesh=mesh, in_specs=in_specs, out_specs=P("span", "tensor"), check_vma=False)
```

time: 100 us -> 41.4 us (0.41)
  the two profiles are of different devices: /device:TPU:7 before, /device:TPU:5 now
where the time goes in v3:
time: 41.4 us; the launch traced here: 40.9 us
  Pallas kernels  32.2 us (78%)
  local copies, waits for them, and re-layouts  8.61 us (21%)
    pallas_call x1, Pallas kernels, layer(): pl.pallas_call(functools.partial(layer_kernel, count, chips), out_shape=j...  32.2 us
    unnamed x25, local copies, waits for them, and re-layouts  8.61 us

profile of v3, /device:TPU:5, one launch (start us, length us, event | category | flops | bytes accessed | tf_op | source)
XLA Modules:
  0.0 40.9 jit_solution(4771261995997452875)
XLA Ops:
  0.0 0.0 copy-start.9
  0.0 0.0 copy-start.7
  0.0 0.0 copy-start.8
  0.0 0.0 copy-start.11
  0.0 0.7 %copy-done.9 = f32[512]{0:T(512)S(1)} copy-done((f32[512]{0:T(512)S(1)}, f32[512]{0:T(512)}, u32[]{:S(2)}) %copy-start.9) | copy-done | bytes 2072
  0.7 0.0 copy-done.7
  0.7 0.0 copy-done.8
  0.7 0.0 copy-done.11
  0.7 0.0 copy-start
  0.7 1.2 %copy-done = bf16[512,1024]{1,0:T(8,128)(2,1)S(1)} copy-done((bf16[512,1024]{1,0:T(8,128)(2,1)S(1)}, bf16[512,1024]{1,0:T(8,128)(2,1)}, u32[]{:S(2)}) %copy-start) | copy-done | bytes 1048600
  2.0 0.0 copy-start.1
  2.0 1.2 %copy-done.1 = bf16[1024,512]{1,0:T(8,128)(2,1)S(1)} copy-done((bf16[1024,512]{1,0:T(8,128)(2,1)S(1)}, bf16[1024,512]{1,0:T(8,128)(2,1)}, u32[]{:S(2)}) %copy-start.1) | copy-done | bytes 1048600
  3.2 0.0 copy-start.2
  3.2 0.9 %copy-done.2 = bf16[256,512]{1,0:T(8,128)(2,1)S(1)} copy-done((bf16[256,512]{1,0:T(8,128)(2,1)S(1)}, bf16[256,512]{1,0:T(8,128)(2,1)}, u32[]{:S(2)}) %copy-start.2) | copy-done | bytes 262168
  4.1 0.0 copy-start.3
  4.1 0.8 %copy-done.3 = f32[2,16,512]{2,1,0:T(8,128)S(1)} copy-done((f32[2,16,512]{2,1,0:T(8,128)S(1)}, f32[2,16,512]{2,1,0:T(8,128)}, u32[]{:S(2)}) %copy-start.3) | copy-done | bytes 65560
  5.0 0.0 copy-start.4
  5.0 0.8 %copy-done.4 = f32[16,512]{1,0:T(8,128)S(1)} copy-done((f32[16,512]{1,0:T(8,128)S(1)}, f32[16,512]{1,0:T(8,128)}, u32[]{:S(2)}) %copy-start.4) | copy-done | bytes 32792
  5.7 0.0 copy-start.5
  5.7 0.8 %copy-done.5 = f32[16,512]{1,0:T(8,128)S(1)} copy-done((f32[16,512]{1,0:T(8,128)S(1)}, f32[16,512]{1,0:T(8,128)}, u32[]{:S(2)}) %copy-start.5) | copy-done | bytes 32792
  6.5 0.0 copy-start.6
  6.5 0.8 %copy-done.6 = f32[16,512]{1,0:T(8,128)S(1)} copy-done((f32[16,512]{1,0:T(8,128)S(1)}, f32[16,512]{1,0:T(8,128)}, u32[]{:S(2)}) %copy-start.6) | copy-done | bytes 32792
  7.2 0.0 copy-start.10
  7.2 0.7 %copy-done.10 = f32[512]{0:T(512)S(1)} copy-done((f32[512]{0:T(512)S(1)}, f32[512]{0:T(512)}, u32[]{:S(2)}) %copy-start.10) | copy-done | bytes 2072
  7.9 32.2 %layer.1 = bf16[4,64,512]{2,1,0:T(8,128)(2,1)S(1)} custom-call(bf16[256,512]{1,0:T(8,128)(2,1)S(1)} %copy-done.2, f32[1,256]{1,0:T(1,128)S(1)} %bitcast.11, f32[1,512]{1,0:T(1,128)S(1)} %bitcast.8, f32[1,512]{1,0:T(1,128)S(1)} %bitcast.9, f32[16,512]{1,0:T(8,128)S(1)} %copy-done.4, f32[16,512]{1,0:T(8,128)S(1)} %copy-done.5, f32[16,512]{1,0:T(8,128)S(1)} %copy-done.6, ...), custom_call_target="tpu_custom_call" | custom-call | tf_op jit(solution)/shard_map/layer/pallas_call | solution.py:391
  40.2 0.7 %copy.14 = bf16[256,512]{1,0:T(8,128)(2,1)} copy(bf16[256,512]{1,0:T(8,128)(2,1)S(1)} %bitcast.6) | data formatting | bytes 524288
Async XLA Ops:
  0.0 0.7 %copy-start.9 = (f32[512]{0:T(512)S(1)}, f32[512]{0:T(512)}, u32[]{:S(2)}) copy-start(f32[512]{0:T(512)} %param.15) | copy-start | bytes 6148
  0.0 0.7 %copy-start.7 = (f32[1024]{0:T(1024)S(1)}, f32[1024]{0:T(1024)}, u32[]{:S(2)}) copy-start(f32[1024]{0:T(1024)} %param.22) | copy-start | bytes 12292
  0.0 0.7 %copy-start.8 = (f32[512]{0:T(512)S(1)}, f32[512]{0:T(512)}, u32[]{:S(2)}) copy-start(f32[512]{0:T(512)} %param.14) | copy-start | bytes 6148
  0.0 0.7 %copy-start.11 = (f32[256]{0:T(256)S(1)}, f32[256]{0:T(256)}, u32[]{:S(2)}) copy-start(f32[256]{0:T(256)} %param.13) | copy-start | bytes 3076
  0.7 1.2 %copy-start = (bf16[512,1024]{1,0:T(8,128)(2,1)S(1)}, bf16[512,1024]{1,0:T(8,128)(2,1)}, u32[]{:S(2)}) copy-start(bf16[512,1024]{1,0:T(8,128)(2,1)} %weight_hbm.1) | copy-start | bytes 3145732
  2.0 1.2 %copy-start.1 = (bf16[1024,512]{1,0:T(8,128)(2,1)S(1)}, bf16[1024,512]{1,0:T(8,128)(2,1)}, u32[]{:S(2)}) copy-start(bf16[1024,512]{1,0:T(8,128)(2,1)} %mixer_hbm.1) | copy-start | bytes 3145732
  3.2 0.9 %copy-start.2 = (bf16[256,512]{1,0:T(8,128)(2,1)S(1)}, bf16[256,512]{1,0:T(8,128)(2,1)}, u32[]{:S(2)}) copy-start(bf16[256,512]{1,0:T(8,128)(2,1)} %tokens_ref.1) | copy-start | bytes 786436
  4.1 0.8 %copy-start.3 = (f32[2,16,512]{2,1,0:T(8,128)S(1)}, f32[2,16,512]{2,1,0:T(8,128)}, u32[]{:S(2)}) copy-start(f32[2,16,512]{2,1,0:T(8,128)} %output_ref.1) | copy-start | bytes 196612
  5.0 0.8 %copy-start.4 = (f32[16,512]{1,0:T(8,128)S(1)}, f32[16,512]{1,0:T(8,128)}, u32[]{:S(2)}) copy-start(f32[16,512]{1,0:T(8,128)} %rate_ref.1) | copy-start | bytes 98308
  5.7 0.8 %copy-start.5 = (f32[16,512]{1,0:T(8,128)S(1)}, f32[16,512]{1,0:T(8,128)}, u32[]{:S(2)}) copy-start(f32[16,512]{1,0:T(8,128)} %angle_ref.1) | copy-start | bytes 98308
  6.5 0.8 %copy-start.6 = (f32[16,512]{1,0:T(8,128)S(1)}, f32[16,512]{1,0:T(8,128)}, u32[]{:S(2)}) copy-start(f32[16,512]{1,0:T(8,128)} %input_ref.1) | copy-start | bytes 98308
  7.2 0.7 %copy-start.10 = (f32[512]{0:T(512)S(1)}, f32[512]{0:T(512)}, u32[]{:S(2)}) copy-start(f32[512]{0:T(512)} %param.20) | copy-start | bytes 6148

commit v4 on v3

--- a/solution.py
+++ b/solution.py
@@ -136,7 +136,7 @@
     length, channels = tokens_ref.shape
     ndim = rate_ref.shape[0]
     blocks = length // STEPS
-    rows = part_ref.shape[2]
+    halves, rows = part_ref.shape[2:4]
     span = lax.axis_index("span")
     me = lax.axis_index("tensor")
     core = lax.rem(me, 2)
@@ -246,16 +246,15 @@
             start_ref[1, block, :, lanes] = im
             first = pl.multiple_of(block * STEPS, STEPS)
             factor = wide(prefix_ref[pl.ds(first + STEPS - 1, 1), :], width)
-            next_re = (whole_re * re - whole_im * im) * factor
-            next_im = (whole_re * im + whole_im * re) * factor
-            for step in range(STEPS):
+            add_re = jnp.broadcast_to(scaled_ref[pl.ds(first + STEPS - 1, 1), lanes], (ndim, width))
+            add_im = jnp.zeros((ndim, width), jnp.float32)
+            for step in range(STEPS - 1):
                 entry = scaled_ref[pl.ds(first + step, 1), lanes]
                 lag = STEPS - 1 - step
-                if lag:
-                    next_re = next_re + power_ref[0, lag, :, lanes] * entry
-                    next_im = next_im + power_ref[1, lag, :, lanes] * entry
-                else:
-                    next_re = next_re + entry
+                add_re = add_re + power_ref[0, lag, :, lanes] * entry
+                add_im = add_im + power_ref[1, lag, :, lanes] * entry
+            next_re = (whole_re * re - whole_im * im) * factor + add_re
+            next_im = (whole_re * im + whole_im * re) * factor + add_im
             return next_re, next_im, kept * factor
 
         zero = jnp.zeros((ndim, width), jnp.float32)
@@ -294,16 +293,8 @@
     for lanes in lanes_of(channels, width):
         whole_re, whole_im = power_ref[0, STEPS, :, lanes], power_ref[1, STEPS, :, lanes]
 
-        def arrive(block, carried):
+        def leave(block, carried):
             re, im = carried
-            start_ref[0, block, :, lanes] += re
-            start_ref[1, block, :, lanes] += im
-            factor = wide(prefix_ref[pl.ds(block * STEPS + STEPS - 1, 1), :], width)
-            return (whole_re * re - whole_im * im) * factor, (whole_re * im + whole_im * re) * factor
-
-        lax.fori_loop(0, blocks, arrive, (power_ref[0, 0, :, lanes], power_ref[1, 0, :, lanes]))
-
-        def leave(block, carried):
             first = pl.multiple_of(block * STEPS, STEPS)
             parts = [jnp.zeros((STEPS, width), jnp.float32) for _ in range(4)]
             for part in range(ndim):
@@ -313,9 +304,18 @@
                 parts[slot + 1] = parts[slot + 1] + read_ref[1, part, :, lanes] * start_ref[1, block, here, lanes]
             read = (parts[0] - parts[1]) + (parts[2] - parts[3])
             ema_ref[pl.ds(first, STEPS), lanes] += read * wide(prefix_ref[pl.ds(first, STEPS), :], width)
-            return carried
-
-        lax.fori_loop(0, blocks, leave, 0)
+            factor = wide(prefix_ref[pl.ds(first + STEPS - 1, 1), :], width)
+            re, im = (whole_re * re - whole_im * im) * factor, (whole_re * im + whole_im * re) * factor
+            start_ref[0, block + 1, :, lanes] += re
+            start_ref[1, block + 1, :, lanes] += im
+            return re, im
+
+        re, im = power_ref[0, 0, :, lanes], power_ref[1, 0, :, lanes]
+        start_ref[0, 0, :, lanes] += re
+        start_ref[1, 0, :, lanes] += im
+        start_ref[0, blocks, :, lanes] = re
+        start_ref[1, blocks, :, lanes] = im
+        lax.fori_loop(0, blocks, leave, (re, im))
 
     ema = ema_ref[...]
     active = (ema / (1.0 + jnp.exp(-ema))).astype(jnp.bfloat16)
@@ -324,57 +324,67 @@
     product = dot(active, weight_ref[...]).astype(jnp.bfloat16)
     part_ref[...] = product.reshape(part_ref.shape)
 
-    pair = []
-    for slot, place in enumerate(order):
-        copy = remote(part_ref.at[place, 1 - core], near_ref.at[slot], pair_send.at[slot], pair_recv.at[slot], "tensor", partner)
+    pair, far, outward, home, back = {}, {}, {}, {}, {}
+    for half in range(halves):
+        for slot, place in enumerate(order):
+            copy = remote(part_ref.at[place, 1 - core, half], near_ref.at[slot, half], pair_send.at[slot, half], pair_recv.at[slot, half], "tensor", partner)
+            copy.start()
+            pair[slot, half] = copy
+    for half in range(halves):
+        for slot, place in enumerate(order[:-1]):
+            pair[slot, half].wait_recv()
+            added = part_ref[place, core, half].astype(jnp.float32) + near_ref[slot, half].astype(jnp.float32)
+            sum_ref[slot, half] = added.astype(jnp.bfloat16)
+            copy = remote(sum_ref.at[slot, half], far_ref.at[slot, half], far_send.at[slot, half], far_recv.at[slot, half], "tensor", peers[slot])
+            copy.start()
+            far[slot, half] = copy
+    for half in range(halves):
+        pair[chips - 1, half].wait_recv()
+        shared = part_ref[chip, core, half].astype(jnp.float32) + near_ref[chips - 1, half].astype(jnp.float32)
+        for slot in range(chips - 1):
+            far[slot, half].wait_recv()
+            shared = shared + far_ref[slot, half].astype(jnp.float32)
+        squares = jnp.mean(shared * shared, axis=1, keepdims=True)
+        own_ref[half] = (shared * lax.rsqrt(squares + SCALE_EPS) * gain_ref[...]).astype(jnp.bfloat16)
+        landing = all_ref.at[chip, core, half]
+        for slot in range(chips - 1):
+            copy = remote(own_ref.at[half], landing, out_send.at[slot, half], out_recv.at[slot, half], "tensor", peers[slot])
+            copy.start()
+            outward[slot, half] = copy
+        copy = remote(own_ref.at[half], landing, back_send.at[chips - 1, half], back_recv.at[chips - 1, half], "tensor", partner)
         copy.start()
-        pair.append(copy)
-    far = []
-    for slot, place in enumerate(order[:-1]):
-        pair[slot].wait_recv()
-        added = part_ref[place, core].astype(jnp.float32) + near_ref[slot].astype(jnp.float32)
-        sum_ref[slot] = added.astype(jnp.bfloat16)
-        copy = remote(sum_ref.at[slot], far_ref.at[slot], far_send.at[slot], far_recv.at[slot], "tensor", peers[slot])
-        copy.start()
-        far.append(copy)
-    pair[-1].wait_recv()
-    shared = part_ref[chip, core].astype(jnp.float32) + near_ref[chips - 1].astype(jnp.float32)
-    for slot in range(chips - 1):
-        far[slot].wait_recv()
-        shared = shared + far_ref[slot].astype(jnp.float32)
-    squares = jnp.mean(shared * shared, axis=1, keepdims=True)
-    own_ref[...] = (shared * lax.rsqrt(squares + SCALE_EPS) * gain_ref[...]).astype(jnp.bfloat16)
-    outward = []
-    for slot in range(chips - 1):
-        copy = remote(own_ref, all_ref.at[chip, core], out_send.at[slot], out_recv.at[slot], "tensor", peers[slot])
-        copy.start()
-        outward.append(copy)
-    home = remote(own_ref, all_ref.at[chip, core], back_send.at[chips - 1], back_recv.at[chips - 1], "tensor", partner)
-    home.start()
-    all_ref[chip, core] = own_ref[...]
-    columns = all_ref.shape[3]
+        home[half] = copy
+        all_ref[chip, core, half] = own_ref[half]
+    columns = all_ref.shape[4]
 
     def finish(place):
-        gathered = all_ref[place].reshape(2 * rows, columns)
+        gathered = all_ref[place].reshape(2 * halves * rows, columns)
         out_ref[place] = dot(gathered, mixer_ref[...]).astype(jnp.bfloat16)
 
-    home.wait_recv()
+    def origin(slot):
+        return lax.rem(chip + chips - 1 - slot, chips)
+
+    def close(slot):
+        for half in range(halves):
+            back[slot, half].wait_recv()
+        finish(origin(slot))
+
+    for half in range(halves):
+        home[half].wait_recv()
     finish(chip)
-    back = []
-    for slot in range(chips - 1):
-        origin = lax.rem(chip + chips - 1 - slot, chips)
-        outward[slot].wait_recv()
-        block = all_ref.at[origin, core]
-        copy = remote(block, block, back_send.at[slot], back_recv.at[slot], "tensor", partner)
-        copy.start()
-        back.append(copy)
-        if slot:
-            back[slot - 1].wait_recv()
-            finish(lax.rem(chip + chips - slot, chips))
-    back[-1].wait_recv()
-    finish(lax.rem(chip + 1, chips))
-    for copy in pair + far + outward + back + [home]:
-        copy.wait_send()
+    for half in range(halves):
+        for slot in range(chips - 1):
+            outward[slot, half].wait_recv()
+            block = all_ref.at[origin(slot), core, half]
+            copy = remote(block, block, back_send.at[slot, half], back_recv.at[slot, half], "tensor", partner)
+            copy.start()
+            back[slot, half] = copy
+            if slot and half == halves - 1:
+                close(slot - 1)
+    close(chips - 2)
+    for copies in (pair, far, outward, home, back):
+        for copy in copies.values():
+            copy.wait_send()
 
 
 def layer(tokens, retain, norm_gain, norm_bias, rate, angle, source, output, skip, weight, gain, mixer):
@@ -384,7 +394,8 @@
     count = lax.axis_size("span")
     chips = lax.axis_size("tensor") // 2
     rows, columns = length // (2 * chips), weight.shape[1]
-    block = (rows, columns)
+    halves = 2 if rows % 32 == 0 else 1
+    block = (halves, rows // halves, columns)
     f32, bf16 = jnp.float32, jnp.bfloat16
     sems = pltpu.SemaphoreType.DMA
     hbm = pl.BlockSpec(memory_space=pltpu.HBM)
@@ -405,7 +416,7 @@
             pltpu.VMEM((2, STEPS + 1, ndim, channels), f32),
             pltpu.VMEM((2, ndim, channels), f32),
             pltpu.VMEM((2, ndim, STEPS, channels), f32),
-            pltpu.VMEM((2, blocks, ndim, channels), f32),
+            pltpu.VMEM((2, blocks + 1, ndim, channels), f32),
             pltpu.VMEM((2 * ndim, channels), bf16),
             pltpu.VMEM((count, 2 * ndim, channels), bf16),
             pltpu.VMEM((8, LANES), f32),
@@ -422,16 +433,16 @@
             sems((1, count - 1)),
             sems((2, count - 1)),
             sems((2, count - 1)),
-            sems((chips,)),
-            sems((chips,)),
-            sems((chips - 1,)),
-            sems((chips - 1,)),
-            sems((chips - 1,)),
-            sems((chips - 1,)),
-            sems((chips,)),
-            sems((chips,)),
+            sems((chips, halves)),
+            sems((chips, halves)),
+            sems((chips - 1, halves)),
+            sems((chips - 1, halves)),
+            sems((chips - 1, halves)),
+            sems((chips - 1, halves)),
+            sems((chips, halves)),
+            sems((chips, halves)),
         ],
-        compiler_params=pltpu.CompilerParams(collective_id=0, has_side_effects=True, vmem_limit_bytes=40 << 20),
+        compiler_params=pltpu.CompilerParams(collective_id=0, has_side_effects=True),
         name="layer",
     )(
         tokens,

time: 41.4 us -> 35.5 us (0.86)
  the two profiles are of different devices: /device:TPU:5 before, /device:TPU:7 now
where the time goes in v4:
time: 35.5 us; the launch traced here: 35.4 us
  Pallas kernels  33.7 us (95%)
  local copies, waits for them, and re-layouts  1.67 us (5%)
    pallas_call x1, Pallas kernels, layer(): pl.pallas_call(functools.partial(layer_kernel, count, chips), out_shape=j...  33.7 us
    unnamed x1, local copies, waits for them, and re-layouts  1.67 us

profile of v4, /device:TPU:7, one launch (start us, length us, event | category | flops | bytes accessed | tf_op | source)
XLA Modules:
  0.0 35.4 jit_solution(12652958827753819628)
XLA Ops:
  0.0 33.7 %layer.1 = bf16[4,64,512]{2,1,0:T(8,128)(2,1)} custom-call(bf16[256,512]{1,0:T(8,128)(2,1)} %tokens_ref.1, f32[1,256]{1,0:T(1,128)} %bitcast.11, f32[1,512]{1,0:T(1,128)} %bitcast.8, f32[1,512]{1,0:T(1,128)} %bitcast.9, f32[16,512]{1,0:T(8,128)} %rate_ref.1, f32[16,512]{1,0:T(8,128)} %angle_ref.1, f32[16,512]{1,0:T(8,128)} %input_ref.1, ...), custom_call_target="tpu_custom_call" | custom-call | tf_op jit(solution)/shard_map/layer/pallas_call | solution.py:402
  33.7 1.7 %copy.14 = bf16[256,512]{1,0:T(8,128)(2,1)} copy(bf16[256,512]{1,0:T(8,128)(2,1)} %bitcast.6) | data formatting | bytes 524288

commit v5 on v4

--- a/solution.py
+++ b/solution.py
@@ -236,7 +236,7 @@
     normed_ref[...] = normed
     scaled_ref[...] = normed * wide(suffix, channels)
 
-    width = min(256, channels)
+    width = min(512, channels)
     for lanes in lanes_of(channels, width):
         whole_re, whole_im = power_ref[0, STEPS, :, lanes], power_ref[1, STEPS, :, lanes]
 
@@ -290,6 +290,7 @@
             power_ref[0, 0] = (by_re * re - by_im * im) * kept + states_ref[other, 0:ndim].astype(jnp.float32)
             power_ref[1, 0] = (by_re * im + by_im * re) * kept + states_ref[other, ndim : 2 * ndim].astype(jnp.float32)
 
+    width = min(256, channels)
     for lanes in lanes_of(channels, width):
         whole_re, whole_im = power_ref[0, STEPS, :, lanes], power_ref[1, STEPS, :, lanes]
 
@@ -315,7 +316,7 @@
         start_ref[1, 0, :, lanes] += im
         start_ref[0, blocks, :, lanes] = re
         start_ref[1, blocks, :, lanes] = im
-        lax.fori_loop(0, blocks, leave, (re, im))
+        lax.fori_loop(0, blocks, leave, (re, im), unroll=2)
 
     ema = ema_ref[...]
     active = (ema / (1.0 + jnp.exp(-ema))).astype(jnp.bfloat16)

time: 35.5 us -> 34.5 us (0.972)
  Pallas kernels: 33.7 us -> 32.7 us
    pallas_call x1, Pallas kernels: 33.7 us -> 32.7 us  [layer(): pl.pallas_call(functools.partial(layer_kernel, count, chips), out_shape=j...]
where the time goes in v5:
time: 34.5 us; the launch traced here: 34.4 us
  Pallas kernels  32.7 us (95%)
  local copies, waits for them, and re-layouts  1.67 us (5%)
    pallas_call x1, Pallas kernels, layer(): pl.pallas_call(functools.partial(layer_kernel, count, chips), out_shape=j...  32.7 us
    unnamed x1, local copies, waits for them, and re-layouts  1.67 us

profile of v5, /device:TPU:7, one launch (start us, length us, event | category | flops | bytes accessed | tf_op | source)
XLA Modules:
  0.0 34.4 jit_solution(10394980867672707252)
XLA Ops:
  0.0 32.7 %layer.1 = bf16[4,64,512]{2,1,0:T(8,128)(2,1)} custom-call(bf16[256,512]{1,0:T(8,128)(2,1)} %tokens_ref.1, f32[1,256]{1,0:T(1,128)} %bitcast.11, f32[1,512]{1,0:T(1,128)} %bitcast.8, f32[1,512]{1,0:T(1,128)} %bitcast.9, f32[16,512]{1,0:T(8,128)} %rate_ref.1, f32[16,512]{1,0:T(8,128)} %angle_ref.1, f32[16,512]{1,0:T(8,128)} %input_ref.1, ...), custom_call_target="tpu_custom_call" | custom-call | tf_op jit(solution)/shard_map/layer/pallas_call | solution.py:403
  32.7 1.7 %copy.14 = bf16[256,512]{1,0:T(8,128)(2,1)} copy(bf16[256,512]{1,0:T(8,128)(2,1)} %bitcast.6) | data formatting | bytes 524288
